TPU v7x, 1024 devices: a whole 4x8x16 slice. The times are simulated.
1024 devices in a mesh: lat: 32 (over x_hi, z), lon: 32 (over y, x_lo, core).
Axes of the slice: x: 4 (x_hi: 2, x_lo: 2; x = x_hi * 2 + x_lo), y: 8, z: 16, core: 2. Of those that a mesh axis runs over, the one named last changes fastest.
Arguments:
- coarse: bfloat16 [2, 192, 192, 1024], P(None, 'lat', 'lon'), may hold values from -6 to 6
- skip_tokens: bfloat16 [2, 384, 384, 512], P(None, 'lat', 'lon'), may hold values from -40 to 40
- land_sea: int32 [384, 384], P('lat', 'lon'), may hold values from 0 to 2
- surf_table: float32 [3, 512], replicated, may hold values from -5 to 5
- expand_weight: bfloat16 [1024, 2048], replicated, may hold values from -0.1875 to 0.1875
- expand_gain: float32 [512], replicated, may hold values from 0.1 to 1.9
- attn_gain: float32 [512], replicated, may hold values from 0.1 to 1.9
- qkv_weight: bfloat16 [512, 1536], replicated, may hold values from -0.25 to 0.25
- logit_scale: float32 [8], replicated, may hold values from 2 to 20
- out_weight: bfloat16 [512, 512], replicated, may hold values from -0.25 to 0.25
Outputs:
- mixed: float32 [2, 384, 384, 512], P(None, 'lat', 'lon')
All inputs are finite; a program needn't handle non-finite values.
Results may differ from a plain program's by a relative error of at most 0.003.
Values may be sent and summed in bfloat16 or wider, within the bound.
No kernel may reach another device: no remote copies, remote signals or barrier semaphores. Data moves between devices by JAX's collectives and lax.ppermute only.
A program may use at most 32 MiB of HBM per device.

v0:
```python
import jax
import jax.numpy as jnp
from jax import lax
from jax.sharding import PartitionSpec as P

WIN_LAT = 6
WIN_LON = 12
SHIFT_LAT = 3
SHIFT_LON = 6


EPSILON = 1e-05


def from_behind(value, axis, steps):
    count = lax.axis_size(axis)
    pairs = [(source, (source + steps) % count) for source in range(count)]
    return lax.ppermute(value, axis, pairs)


def layer_norm(values, gain_vector):
    average = jnp.mean(values, axis=-1, keepdims=True)
    centred = values - average
    spread = jnp.mean(centred * centred, axis=-1, keepdims=True)
    return centred * lax.rsqrt(spread + EPSILON) * gain_vector


def expand_tokens(coarse, expand_weight, expand_gain):
    levels, height, breadth, channels = coarse.shape
    expanded = jnp.dot(
        coarse.reshape(-1, channels), expand_weight, preferred_element_type=jnp.float32
    )
    expanded = expanded.reshape(levels, height, breadth, 2, 2, -1)
    expanded = jnp.transpose(expanded, (0, 1, 3, 2, 4, 5))
    expanded = expanded.reshape(levels, 2 * height, 2 * breadth, -1)
    return layer_norm(expanded, expand_gain)


def surface_terms(land_sea, surf_table):
    result = jnp.zeros(land_sea.shape + (surf_table.shape[1],), jnp.float32)
    for category in range(surf_table.shape[0]):
        picked = (land_sea == category).astype(jnp.float32)
        result = result + picked[:, :, None] * surf_table[category]
    return result


def window_attention(region, row_group, attn_gain, qkv_weight, logit_scale):
    levels, height, breadth, channels = region.shape
    head_count = logit_scale.shape[0]
    head_width = channels // head_count
    lat_windows = height // WIN_LAT
    lon_windows = breadth // WIN_LON
    window_size = levels * WIN_LAT * WIN_LON
    normed = layer_norm(region.astype(jnp.float32), attn_gain).astype(jnp.bfloat16)
    packed = jnp.dot(
        normed.reshape(-1, channels), qkv_weight, preferred_element_type=jnp.float32
    ).astype(jnp.bfloat16)
    packed = packed.reshape(
        levels, lat_windows, WIN_LAT, lon_windows, WIN_LON, 3, head_count, head_width
    )
    packed = jnp.transpose(packed, (5, 1, 3, 6, 0, 2, 4, 7)).reshape(
        3, lat_windows, lon_windows, head_count, window_size, head_width
    )
    queries = packed[0].astype(jnp.float32)
    key_rows = packed[1].astype(jnp.float32)
    queries = queries * lax.rsqrt(jnp.sum(queries * queries, axis=-1, keepdims=True) + 1e-06)
    key_rows = key_rows * lax.rsqrt(jnp.sum(key_rows * key_rows, axis=-1, keepdims=True) + 1e-06)
    scores = jnp.einsum("abhqe,abhke->abhqk", queries, key_rows, precision=lax.Precision.HIGHEST)
    scores = scores * logit_scale[None, None, :, None, None]
    token_group = jnp.broadcast_to(
        row_group.reshape(1, lat_windows, WIN_LAT, 1), (levels, lat_windows, WIN_LAT, WIN_LON)
    )
    token_group = jnp.transpose(token_group, (1, 0, 2, 3)).reshape(lat_windows, window_size)
    allowed = token_group[:, :, None] == token_group[:, None, :]
    weights = jnp.where(allowed[:, None, None], jnp.exp(scores), jnp.float32(0.0))
    attention = (weights / jnp.sum(weights, axis=-1, keepdims=True)).astype(jnp.bfloat16)
    blended = jnp.einsum(
        "abhqk,abhke->abhqe", attention, packed[2], preferred_element_type=jnp.float32
    ).astype(jnp.bfloat16)
    blended = blended.reshape(
        lat_windows, lon_windows, head_count, levels, WIN_LAT, WIN_LON, head_width
    )
    blended = jnp.transpose(blended, (3, 0, 4, 1, 5, 2, 6)).reshape(
        levels, height, breadth, channels
    )
    return blended


def project(blended, out_weight):
    projected = jnp.dot(
        blended.reshape(-1, blended.shape[-1]), out_weight, preferred_element_type=jnp.float32
    )
    return projected.reshape(blended.shape)


def per_device(
    coarse,
    skip_tokens,
    land_sea,
    surf_table,
    expand_weight,
    expand_gain,
    attn_gain,
    qkv_weight,
    logit_scale,
    out_weight,
):
    fine = expand_tokens(coarse, expand_weight, expand_gain)
    tokens = (
        skip_tokens.astype(jnp.float32) + fine + surface_terms(land_sea, surf_table)[None]
    ).astype(jnp.bfloat16)
    lat_rows = tokens.shape[1]
    lon_cols = tokens.shape[2]
    total_rows = lat_rows * lax.axis_size("lat")
    first_row = lax.axis_index("lat") * lat_rows
    upper = from_behind(tokens[:, :SHIFT_LAT], "lat", -1)
    lat_block = jnp.concatenate((tokens[:, SHIFT_LAT:], upper), axis=1)
    beside = from_behind(lat_block[:, :, :SHIFT_LON], "lon", -1)
    region = jnp.concatenate((lat_block[:, :, SHIFT_LON:], beside), axis=2)
    global_rows = (first_row + SHIFT_LAT + jnp.arange(lat_rows, dtype=jnp.int32)) % total_rows
    row_group = (global_rows - SHIFT_LAT) // WIN_LAT
    blended = window_attention(region, row_group, attn_gain, qkv_weight, logit_scale)
    returned = from_behind(blended[:, :, lon_cols - SHIFT_LON :], "lon", 1)
    lat_order = jnp.concatenate((returned, blended[:, :, : lon_cols - SHIFT_LON]), axis=2)
    lowered = from_behind(lat_order[:, lat_rows - SHIFT_LAT :], "lat", 1)
    own_blended = jnp.concatenate((lowered, lat_order[:, : lat_rows - SHIFT_LAT]), axis=1)
    return tokens.astype(jnp.float32) + project(own_blended, out_weight)


def solution(mesh):
    in_specs = (
        P(None, "lat", "lon", None),
        P(None, "lat", "lon", None),
        P("lat", "lon"),
        P(),
        P(),
        P(),
        P(),
        P(),
        P(),
        P(),
    )
    out_specs = P(None, "lat", "lon", None)
    return jax.shard_map(
        per_device, mesh=mesh, in_specs=in_specs, out_specs=out_specs, check_vma=False
    )
```

profile of v0, /device:TPU:4, one launch (start us, length us, event | category | flops | bytes accessed | tf_op | source)
XLA Modules:
  0.0 78.7 jit_solution(8836202436800627016)
XLA Ops:
  0.0 6.5 %copy.94 = bf16[2048,1024]{1,0:T(8,128)(2,1)} copy(bf16[2048,1024]{0,1:T(8,128)(2,1)} %bitcast.37) | data formatting | bytes 8388608 | tf_op jit(solution)/shard_map/dot_general | solution.py:30
  6.5 3.8 %fusion.28 = (f32[2,6,2,6,2]{3,4,2,1,0:T(2,128)S(1)}, f32[2,6,2,6,2,512]{5,3,4,2,1,0:T(8,128)S(1)}) fusion(bf16[2,2,512,1024,1,1]{3,2,1,0,5,4:T(8,128)(2,1)} %bitcast.38, bf16[2,6,6,1024,1,1]{3,0,2,1,5,4:T(2,128)(2,1)S(1)} %bitcast.45), kind=kOutput, calls=%fused_computation.63 | convolution fusion | flops 302137056 | bytes 4932736 | tf_op jit(solution)/shard_map/dot_general | solution.py:30
  10.4 0.5 copy.66
  12.4 18.2 %collective-permute-start = (bf16[2,3,12,512]{3,2,1,0:T(8,128)(2,1)S(1)}, bf16[2,3,12,512]{3,2,1,0:T(8,128)(2,1)S(1)}, u32[]{:S(2)}, u32[]{:S(2)}) collective-permute-start(bf16[2,3,12,512]{3,2,1,0:T(8,128)(2,1)S(1)} %slice.60), channel_id=1, source_target_pairs={{0,992},{32,0},{64,32},{96,64},{128,96},{160,128},{192,160},{224,1... | collective-permute-start | bytes 221192 | tf_op jit(solution)/shard_map/ppermute | solution.py:18
  30.8 2.0 %collective-permute-done = bf16[2,3,12,512]{3,2,1,0:T(8,128)(2,1)S(1)} collective-permute-done((bf16[2,3,12,512]{3,2,1,0:T(8,128)(2,1)S(1)}, bf16[2,3,12,512]{3,2,1,0:T(8,128)(2,1)S(1)}, u32[]{:S(2)}, u32[]{:S(2)}) %collective-permute-start) | collective-permute-done | bytes 73760 | tf_op jit(solution)/shard_map/ppermute | solution.py:18
  32.9 5.5 %collective-permute-start.1 = (bf16[2,12,6,512]{3,2,1,0:T(8,128)(2,1)S(1)}, bf16[2,12,6,512]{3,2,1,0:T(8,128)(2,1)S(1)}, u32[]{:S(2)}, u32[]{:S(2)}) collective-permute-start(bf16[2,12,6,512]{3,2,1,0:T(8,128)(2,1)S(1)} %get-tuple-element.13), channel_id=1, source_target_pairs={{0,31},{1,0},{2,1},{3,2},{4,3},{5,4},{6,5},{7,6},{8,7},{9,8},{10,9... | collective-permute-start | bytes 442376 | tf_op jit(solution)/shard_map/ppermute | solution.py:18
  38.5 3.0 %collective-permute-done.1 = bf16[2,12,6,512]{3,2,1,0:T(8,128)(2,1)S(1)} collective-permute-done((bf16[2,12,6,512]{3,2,1,0:T(8,128)(2,1)S(1)}, bf16[2,12,6,512]{3,2,1,0:T(8,128)(2,1)S(1)}, u32[]{:S(2)}, u32[]{:S(2)}) %collective-permute-start.1) | collective-permute-done | bytes 147488 | tf_op jit(solution)/shard_map/ppermute | solution.py:18
  41.9 0.3 multiply_reduce_fusion.2
  42.5 1.6 %convolution_convert_fusion = bf16[288,1536]{1,0:T(8,128)(2,1)} fusion(bf16[512,1536]{1,0:T(8,128)(2,1)S(1)} %copy-done, f32[288,512]{1,0:T(8,128)S(1)} %reshape.212, f32[512]{0:T(512)S(1)} %copy-done.10, f32[288]{0:T(512)S(1)} %rsqrt.47, f32[288]{0:T(512)S(1)} %div.40), kind=kOutput, calls=%fused_computation | convolution fusion | flops 454017024 | bytes 3051776 | tf_op jit(solution)/shard_map/dot_general | solution.py:55
  44.1 2.6 %reshape.208 = bf16[2,2,6,1,12,3,8,64]{7,6,5,4,2,1,0,3:T(8,128)(2,1)S(1)} reshape(bf16[288,1536]{1,0:T(8,128)(2,1)} %convolution_convert_fusion) | data formatting | bytes 1769472 | tf_op jit(solution)/shard_map/reshape | solution.py:58
  46.7 0.4 copy.128
  47.1 1.4 %fusion.25 = (bf16[1,2,1,8,2,6,12,64]{7,3,6,5,4,1,2,0:T(8,128)(2,1)}, f32[1,2,1,8,2,6,12,64]{7,3,6,5,4,1,2,0:T(8,128)S(1)}, f32[1,2,1,8,2,6,12,64]{7,3,6,5,4,1,2,0:T(8,128)}) fusion(bf16[3,2,1,8,2,6,12,64]{7,3,6,5,4,1,2,0:T(8,128)(2,1)S(1)} %bitcast.33), kind=kLoop, calls=%fused_computation.60 | loop fusion | flops 294912 | bytes 2359296 | tf_op jit(solution)/shard_map/slice | solution.py:78
  48.5 0.7 multiply_reduce_fusion.1
  50.3 1.9 %broadcast_multiply_fusion = (f32[2,8,144,64]{3,1,2,0:T(8,128)S(1)}, f32[2,8,144,64]{3,1,2,0:T(8,128)S(1)}) fusion(f32[2,8,144,64]{3,1,2,0:T(8,128)S(1)} %bitcast.35, f32[2,8,144]{1,2,0:T(8,128)S(1)} %copy.78, f32[2,8,144,64]{3,1,2,0:T(8,128)} %bitcast.36, f32[2,8,144]{1,2,0:T(8,128)S(1)} %copy.75), kind=kLoop, calls=%fused_computation.25 | loop fusion | flops 294912 | bytes 2377728 | tf_op jit(solution)/shard_map/mul | solution.py:67
  52.2 2.7 %fusion = (f32[2,8,144]{2,1,0:T(8,128)S(1)}, f32[2,8,144,144]{2,3,1,0:T(8,128)S(1)}) fusion(f32[8]{0:T(128)S(1)} %copy-done.8, pred[2,144,144]{1,2,0:T(8,128)(4,1)S(1)} %broadcast_compare_fusion, f32[2,8,144,64]{3,1,2,0:T(8,128)S(1)} %get-tuple-element.24, f32[2,8,144,64]{3,1,2,0:T(8,128)S(1)} %get-tuple-element.25), kind=kOutput, calls=%fused_computation.3 | convolution fusion | flops 255796992 | bytes 2557472 | tf_op jit(solution)/shard_map/abhqe,abhke->abhqk/dot_general | solution.py:68
  54.9 0.8 convolution_convert_fusion.1
  55.7 0.4 copy.83
  56.1 0.4 reshape.220
  56.6 1.9 %collective-permute-start.2 = (bf16[2,12,6,512]{3,2,1,0:T(8,128)(2,1)S(1)}, bf16[2,12,6,512]{3,2,1,0:T(8,128)(2,1)S(1)}, u32[]{:S(2)}, u32[]{:S(2)}) collective-permute-start(bf16[2,12,6,512]{3,2,1,0:T(8,128)(2,1)S(1)} %get-tuple-element.10), channel_id=1, source_target_pairs={{0,1},{1,2},{2,3},{3,4},{4,5},{5,6},{6,7},{7,8},{8,9},{9,10},{10,1... | collective-permute-start | bytes 442376 | tf_op jit(solution)/shard_map/ppermute | solution.py:18
  58.5 7.3 %collective-permute-done.2 = bf16[2,12,6,512]{3,2,1,0:T(8,128)(2,1)S(1)} collective-permute-done((bf16[2,12,6,512]{3,2,1,0:T(8,128)(2,1)S(1)}, bf16[2,12,6,512]{3,2,1,0:T(8,128)(2,1)S(1)}, u32[]{:S(2)}, u32[]{:S(2)}) %collective-permute-start.2) | collective-permute-done | bytes 147488 | tf_op jit(solution)/shard_map/ppermute | solution.py:18
  65.9 1.9 %collective-permute-start.3 = (bf16[2,3,12,512]{3,2,1,0:T(8,128)(2,1)S(1)}, bf16[2,3,12,512]{3,2,1,0:T(8,128)(2,1)S(1)}, u32[]{:S(2)}, u32[]{:S(2)}) collective-permute-start(bf16[2,3,12,512]{3,2,1,0:T(8,128)(2,1)S(1)} %pad_maximum_fusion.2), channel_id=1, source_target_pairs={{0,32},{32,64},{64,96},{96,128},{128,160},{160,192},{192,224},{224... | collective-permute-start | bytes 221192 | tf_op jit(solution)/shard_map/ppermute | solution.py:18
  67.8 8.2 %collective-permute-done.3 = bf16[2,3,12,512]{3,2,1,0:T(8,128)(2,1)S(1)} collective-permute-done((bf16[2,3,12,512]{3,2,1,0:T(8,128)(2,1)S(1)}, bf16[2,3,12,512]{3,2,1,0:T(8,128)(2,1)S(1)}, u32[]{:S(2)}, u32[]{:S(2)}) %collective-permute-start.3) | collective-permute-done | bytes 73760 | tf_op jit(solution)/shard_map/ppermute | solution.py:18
  76.0 1.4 %convolution_add_fusion = f32[2,12,12,512]{3,2,1,0:T(8,128)S(1)} fusion(bf16[2,12,12,512]{3,2,1,0:T(8,128)(2,1)S(1)} %copy-done.2, bf16[512,512]{1,0:T(8,128)(2,1)} %param.19, bf16[2,12,6,512]{3,2,1,0:T(8,128)(2,1)S(1)} %get-tuple-element.11, bf16[2,12,6,512]{3,2,1,0:T(8,128)(2,1)S(1)} %collective-permute-done.2, ...), kind=kOutput, calls=%fused_computation.5 | convolution fusion | flops 152174592 | bytes 1777664 | tf_op jit(solution)/shard_map/dot_general | solution.py:90
  77.5 1.3 %copy.87 = f32[2,12,12,512]{3,0,2,1:T(2,128)} copy(f32[2,12,12,512]{3,2,1,0:T(8,128)S(1)} %convolution_add_fusion) | data formatting | bytes 1179648 | tf_op jit(solution)/shard_map/add | solution.py:127
  (60 shorter events, 3.6 us)
Async XLA Ops:
  0.0 42.5 %copy-start = (bf16[512,1536]{1,0:T(8,128)(2,1)S(1)}, bf16[512,1536]{1,0:T(8,128)(2,1)}, u32[]{:S(2)}) copy-start(bf16[512,1536]{1,0:T(8,128)(2,1)} %param.17) | copy-start | bytes 4718596
  0.0 6.5 %copy-start.9 = (bf16[2,6,6,1024]{3,0,2,1:T(2,128)(2,1)S(1)}, bf16[2,6,6,1024]{3,0,2,1:T(2,128)(2,1)}, u32[]{:S(2)}) copy-start(bf16[2,6,6,1024]{3,0,2,1:T(2,128)(2,1)} %param.10) | copy-start | bytes 442372
  10.4 1.1 %copy-start.5 = (s32[12,12]{1,0:T(8,128)S(1)}, s32[12,12]{1,0:T(8,128)}, u32[]{:S(2)}) copy-start(s32[12,12]{1,0:T(8,128)} %param.12) | copy-start | bytes 1732
  10.4 1.1 %copy-start.6 = (f32[3,512]{1,0:T(4,128)S(1)}, f32[3,512]{1,0:T(4,128)}, u32[]{:S(2)}) copy-start(f32[3,512]{1,0:T(4,128)} %param.13) | copy-start | bytes 18436
  10.4 1.7 %copy-start.4 = (bf16[2,12,12,512]{3,0,2,1:T(2,128)(2,1)S(1)}, bf16[2,12,12,512]{3,0,2,1:T(2,128)(2,1)}, u32[]{:S(2)}) copy-start(bf16[2,12,12,512]{3,0,2,1:T(2,128)(2,1)} %param.11) | copy-start | bytes 884740
  10.4 1.7 %copy-start.7 = (f32[512]{0:T(512)S(1)}, f32[512]{0:T(512)}, u32[]{:S(2)}) copy-start(f32[512]{0:T(512)} %param.15) | copy-start | bytes 6148
  12.4 18.2 %copy-start.1 = (bf16[2,12,12,512]{3,2,1,0:T(8,128)(2,1)}, bf16[2,12,12,512]{3,2,1,0:T(8,128)(2,1)S(1)}, u32[]{:S(2)}) copy-start(bf16[2,12,12,512]{3,2,1,0:T(8,128)(2,1)S(1)} %fusion.9) | copy-start | bytes 884740
  12.4 20.4 %collective-permute-start = (bf16[2,3,12,512]{3,2,1,0:T(8,128)(2,1)S(1)}, bf16[2,3,12,512]{3,2,1,0:T(8,128)(2,1)S(1)}, u32[]{:S(2)}, u32[]{:S(2)}) collective-permute-start(bf16[2,3,12,512]{3,2,1,0:T(8,128)(2,1)S(1)} %slice.60), channel_id=1, source_target_pairs={{0,992},{32,0},{64,32},{96,64},{128,96},{160,128},{192,160},{224,1... | collective-permute-start | bytes 221192 | tf_op jit(solution)/shard_map/ppermute | solution.py:18
  32.9 8.7 %collective-permute-start.1 = (bf16[2,12,6,512]{3,2,1,0:T(8,128)(2,1)S(1)}, bf16[2,12,6,512]{3,2,1,0:T(8,128)(2,1)S(1)}, u32[]{:S(2)}, u32[]{:S(2)}) collective-permute-start(bf16[2,12,6,512]{3,2,1,0:T(8,128)(2,1)S(1)} %get-tuple-element.13), channel_id=1, source_target_pairs={{0,31},{1,0},{2,1},{3,2},{4,3},{5,4},{6,5},{7,6},{8,7},{9,8},{10,9... | collective-permute-start | bytes 442376 | tf_op jit(solution)/shard_map/ppermute | solution.py:18
  41.8 0.8 copy-start.10
  50.2 1.9 %copy-start.8 = (f32[8]{0:T(128)S(1)}, f32[8]{0:T(128)}, u32[]{:S(2)}) copy-start(f32[8]{0:T(128)} %param.18) | copy-start | bytes 100
  52.1 2.8 %copy-start.3 = (bf16[1,2,1,8,2,6,12,64]{7,3,6,5,4,1,2,0:T(8,128)(2,1)S(1)}, bf16[1,2,1,8,2,6,12,64]{7,3,6,5,4,1,2,0:T(8,128)(2,1)}, u32[]{:S(2)}) copy-start(bf16[1,2,1,8,2,6,12,64]{7,3,6,5,4,1,2,0:T(8,128)(2,1)} %get-tuple-element.7) | copy-start | bytes 884740
  56.1 20.0 %copy-start.2 = (bf16[2,12,12,512]{3,2,1,0:T(8,128)(2,1)S(1)}, bf16[2,12,12,512]{3,2,1,0:T(8,128)(2,1)}, u32[]{:S(2)}) copy-start(bf16[2,12,12,512]{3,2,1,0:T(8,128)(2,1)} %copy-done.1) | copy-start | bytes 884740
  56.6 9.3 %collective-permute-start.2 = (bf16[2,12,6,512]{3,2,1,0:T(8,128)(2,1)S(1)}, bf16[2,12,6,512]{3,2,1,0:T(8,128)(2,1)S(1)}, u32[]{:S(2)}, u32[]{:S(2)}) collective-permute-start(bf16[2,12,6,512]{3,2,1,0:T(8,128)(2,1)S(1)} %get-tuple-element.10), channel_id=1, source_target_pairs={{0,1},{1,2},{2,3},{3,4},{4,5},{5,6},{6,7},{7,8},{8,9},{9,10},{10,1... | collective-permute-start | bytes 442376 | tf_op jit(solution)/shard_map/ppermute | solution.py:18
  65.9 10.1 %collective-permute-start.3 = (bf16[2,3,12,512]{3,2,1,0:T(8,128)(2,1)S(1)}, bf16[2,3,12,512]{3,2,1,0:T(8,128)(2,1)S(1)}, u32[]{:S(2)}, u32[]{:S(2)}) collective-permute-start(bf16[2,3,12,512]{3,2,1,0:T(8,128)(2,1)S(1)} %pad_maximum_fusion.2), channel_id=1, source_target_pairs={{0,32},{32,64},{64,96},{96,128},{128,160},{160,192},{192,224},{224... | collective-permute-start | bytes 221192 | tf_op jit(solution)/shard_map/ppermute | solution.py:18
where the time goes:
time: 79.2 us; the launch traced here: 78.7 us
  starting transfers between devices  27.5 us (35%)
  waiting for transfers between devices  20.5 us (26%)
  local copies, waits for them, and re-layouts  14.2 us (18%)
  matrix products  10.3 us (13%)
  other arithmetic  5.65 us (7%)
    ppermute x4, starting transfers between devices, from_behind(): return lax.ppermute(value, axis, pairs)  27.5 us
    ppermute x4, waiting for transfers between devices, from_behind(): return lax.ppermute(value, axis, pairs)  20.5 us
    dot_general x1, local copies, waits for them, and re-layouts, expand_tokens(): jnp.dot(coarse.reshape(-1, channels), expand_weight, preferred_element_ty...  6.54 us
    dot_general x1, matrix products, expand_tokens(): jnp.dot(coarse.reshape(-1, channels), expand_weight, preferred_element_ty...  3.81 us
    reshape x2, local copies, waits for them, and re-layouts, window_attention(): packed.reshape(levels, lat_windows, WIN_LAT, lon_windows, WIN_LON, 3, hea...  2.98 us
    dot_general x1, matrix products, window_attention(): jnp.einsum('abhqe,abhke->abhqk', queries, key_rows, precision=lax.Precisi...  2.75 us
    mul x1, other arithmetic, window_attention(): key_rows * lax.rsqrt(jnp.sum(key_rows * key_rows, axis=-1, keepdims=True)...  1.87 us
    dot_general x1, matrix products, window_attention(): jnp.dot(normed.reshape(-1, channels), qkv_weight, preferred_element_type=...  1.59 us
  transfers between devices with their start and end apart: 4, of which 4 were waited for; matrix products, arithmetic and copies ran while one was open for 0% of the time, Pallas kernels for 0%

commit v1 on v0

v1 whole, which is shorter than its diff:
```python
import functools

import jax
import jax.numpy as jnp
import numpy as np
from jax import lax
from jax.experimental import pallas as pl
from jax.experimental.pallas import tpu as pltpu
from jax.sharding import PartitionSpec as P

D = 512
HEADS = 8
HEAD = 64
ROWS = 12
COLS = 12
Z = 2
EPSILON = 1e-05

HALF = 152
MID, EDGE, EDGE_LIVE = 72, 40, 36
OWN = 2 * HALF


def half_tokens(half):
    columns = range(6 * half, 6 * half + 6)
    listed = []
    for rows, size in ((range(3, 9), MID), (range(0, 3), EDGE), (range(9, 12), EDGE)):
        part = [(r, c, z) for r in rows for c in columns for z in range(Z)]
        listed += part + [None] * (size - len(part))
    return listed


KEPT = half_tokens(0) + half_tokens(1)


def natural(r, c, z):
    return (r * COLS + c) * Z + z


def selections():
    to_phase = np.zeros((4, 72, 288), np.float32)
    to_kept = np.zeros((4, OWN, 72), np.float32)
    to_natural = np.zeros((288, OWN), np.float32)
    for r in range(ROWS):
        for c in range(COLS):
            for z in range(Z):
                phase = 2 * (r % 2) + c % 2
                place = ((r // 2) * 6 + c // 2) * Z + z
                to_phase[phase, place, natural(r, c, z)] = 1.0
                kept = KEPT.index((r, c, z))
                to_kept[phase, kept, place] = 1.0
                to_natural[natural(r, c, z), kept] = 1.0
    return to_phase, to_kept, to_natural


TO_PHASE, TO_KEPT, TO_NATURAL = selections()


def normalized(values, gain):
    average = jnp.mean(values, axis=-1, keepdims=True)
    centred = values - average
    spread = jnp.mean(centred * centred, axis=-1, keepdims=True)
    return centred * lax.rsqrt(spread + EPSILON) * gain


def dot(a, b):
    return jnp.dot(a, b, preferred_element_type=jnp.float32)


def expand_kernel(coarse, weight, skip, surface, table, gain, to_phase, to_kept, out, total):
    phase = pl.program_id(0)
    fine = normalized(dot(coarse[...], weight[...]), gain[...])
    beside = dot(to_phase[0], skip[...])
    kind = surface[0]
    term = jnp.where(kind == 0, table[0:1], jnp.where(kind == 1, table[1:2], table[2:3]))
    tokens = (beside + fine + term).astype(jnp.bfloat16)
    placed = dot(to_kept[0], tokens)

    @pl.when(phase == 0)
    def _():
        total[...] = placed

    @pl.when(phase > 0)
    def _():
        total[...] += placed

    @pl.when(phase == 3)
    def _():
        out[...] = total[...].astype(jnp.bfloat16)


def expand(coarse, skip, land_sea, surf_table, expand_weight, expand_gain):
    rows = jnp.transpose(coarse, (1, 2, 0, 3)).reshape(72, 1024)
    beside = jnp.transpose(skip, (1, 2, 0, 3)).reshape(288, D)
    kinds = jnp.transpose(land_sea.reshape(6, 2, 6, 2), (1, 3, 0, 2)).reshape(4, 36, 1)
    kinds = jnp.broadcast_to(kinds, (4, 36, 2)).reshape(4, 72, 1)
    whole = lambda shape: pl.BlockSpec(shape, lambda i: (0,) * len(shape))
    return pl.pallas_call(
        expand_kernel,
        grid=(4,),
        out_shape=jax.ShapeDtypeStruct((OWN, D), jnp.bfloat16),
        in_specs=[
            whole((72, 1024)),
            pl.BlockSpec((1024, D), lambda i: (0, i)),
            whole((288, D)),
            pl.BlockSpec((1, 72, 1), lambda i: (i, 0, 0)),
            whole((3, D)),
            whole((1, D)),
            pl.BlockSpec((1, 72, 288), lambda i: (i, 0, 0)),
            pl.BlockSpec((1, OWN, 72), lambda i: (i, 0, 0)),
        ],
        out_specs=whole((OWN, D)),
        scratch_shapes=[pltpu.VMEM((OWN, D), jnp.float32)],
        cost_estimate=pl.CostEstimate(flops=2 * 72 * 1024 * 2048, bytes_accessed=5 << 20, transcendentals=0),
        name="expand",
    )(
        rows,
        expand_weight,
        beside,
        kinds,
        surf_table,
        expand_gain.reshape(1, D),
        jnp.asarray(TO_PHASE, jnp.bfloat16),
        jnp.asarray(TO_KEPT, jnp.bfloat16),
    )


PARTS = ((0, MID), (MID, EDGE), (MID + EDGE, EDGE))


def attention_kernel(
    own, left, right, above, below, gain, weight, scale, ones, out_weight, to_natural, out, blended
):
    lat = lax.axis_index("lat")
    last = lax.axis_size("lat") - 1
    bf16 = lambda v: v.astype(jnp.bfloat16)
    pieces, starts, asked = [], [], []
    for half, beside in ((0, left), (1, right)):
        for part, (first, size) in enumerate(PARTS):
            starts.append(sum(p.shape[0] for p in pieces))
            mine = own[half * HALF + first : half * HALF + first + size].astype(jnp.float32)
            window = [mine, beside[first : first + size].astype(jnp.float32)]
            if part:
                outside = above if part == 1 else below
                for side in (0, 1):
                    at = (2 * half + side) * EDGE
                    window.append(outside[at : at + EDGE].astype(jnp.float32))
            window = jnp.concatenate(window, axis=0)
            window = normalized(window, gain[...])
            pieces.append(window)
            asked.append(window[:size])
    every = bf16(jnp.concatenate(pieces, axis=0))
    asking = bf16(jnp.concatenate(asked, axis=0))
    lane = lax.broadcasted_iota(jnp.int32, (1, 256), 1) // HEAD
    for group in (0, 1):
        at = group * 256

        def unit(rows, column, factor):
            product = bf16(dot(rows, weight[:, column : column + 256])).astype(jnp.float32)
            squares = dot(bf16(product * product), ones[...])
            product = product * lax.rsqrt(squares + 1e-06)
            return product if factor is None else product * factor

        queries = unit(asking, at, scale[:, at : at + 256])
        keys = bf16(unit(every, D + at, None))
        values = bf16(dot(every, weight[:, 2 * D + at : 2 * D + at + 256]))
        q_at = 0
        for window in range(6):
            part = window % 3
            size = PARTS[part][1]
            count = 144 if part == 0 else 4 * EDGE
            first = starts[window]
            k = keys[first : first + count]
            v = values[first : first + count]
            q = queries[q_at : q_at + size]
            stacked = bf16(jnp.concatenate([jnp.where(lane == h, q, 0.0) for h in range(4)], axis=0))
            scores = lax.dot_general(stacked, k, (((1,), (1,)), ((), ())), preferred_element_type=jnp.float32)
            powers = jnp.exp(scores)
            if part:
                key = lax.broadcasted_iota(jnp.int32, (1, count), 1)
                inside = lat > 0 if part == 1 else lat < last
                limit = jnp.where(inside, count, 2 * EDGE)
                live = (lax.rem(key, EDGE) < EDGE_LIVE) & (key < limit)
                powers = jnp.where(live, powers, 0.0)
            share = 1.0 / jnp.sum(powers, axis=-1, keepdims=True)
            mixed = dot(bf16(powers), v) * share
            result = jnp.where(lane == 0, mixed[:size], 0.0)
            for h in range(1, 4):
                result = jnp.where(lane == h, mixed[h * size : (h + 1) * size], result)
            blended[q_at : q_at + size, at : at + 256] = result
            q_at += size
    placed = bf16(dot(to_natural[...], bf16(blended[...])))
    tokens = dot(to_natural[...], own[...])
    out[...] = tokens + dot(placed, out_weight[...])


def attention(own, left, right, above, below, attn_gain, qkv_weight, logit_scale, out_weight):
    ones = np.kron(np.eye(4, dtype=np.float32), np.ones((HEAD, HEAD), np.float32))
    return pl.pallas_call(
        attention_kernel,
        out_shape=jax.ShapeDtypeStruct((288, D), jnp.float32),
        in_specs=[pl.BlockSpec(memory_space=pltpu.VMEM)] * 11,
        out_specs=pl.BlockSpec(memory_space=pltpu.VMEM),
        scratch_shapes=[pltpu.VMEM((OWN, D), jnp.float32)],
        cost_estimate=pl.CostEstimate(flops=4 << 30, bytes_accessed=4 << 20, transcendentals=700000),
        name="attention",
    )(
        own,
        left,
        right,
        above,
        below,
        attn_gain.reshape(1, D),
        qkv_weight,
        jnp.repeat(logit_scale, HEAD).reshape(1, D),
        jnp.asarray(ones, jnp.bfloat16),
        out_weight,
        jnp.asarray(TO_NATURAL, jnp.bfloat16),
    )


def shifted(value, axis, steps, wrap):
    count = lax.axis_size(axis)
    pairs = [(source, (source + steps) % count) for source in range(count) if wrap or 0 <= source + steps < count]
    return lax.ppermute(value, axis, pairs)


def per_device(
    coarse,
    skip_tokens,
    land_sea,
    surf_table,
    expand_weight,
    expand_gain,
    attn_gain,
    qkv_weight,
    logit_scale,
    out_weight,
):
    own = expand(coarse, skip_tokens, land_sea, surf_table, expand_weight, expand_gain)
    right = shifted(own[:HALF], "lon", -1, True)
    left = shifted(own[HALF:], "lon", 1, True)
    parts = (own[:HALF], left, own[HALF:], right)
    top = jnp.concatenate([p[MID : MID + EDGE] for p in parts], axis=0)
    bottom = jnp.concatenate([p[MID + EDGE :] for p in parts], axis=0)
    below = shifted(top, "lat", -1, False)
    above = shifted(bottom, "lat", 1, False)
    mixed = attention(own, left, right, above, below, attn_gain, qkv_weight, logit_scale, out_weight)
    return jnp.transpose(mixed.reshape(ROWS, COLS, Z, D), (2, 0, 1, 3))


def solution(mesh):
    in_specs = (
        P(None, "lat", "lon", None),
        P(None, "lat", "lon", None),
        P("lat", "lon"),
        P(),
        P(),
        P(),
        P(),
        P(),
        P(),
        P(),
    )
    out_specs = P(None, "lat", "lon", None)
    return jax.shard_map(
        per_device, mesh=mesh, in_specs=in_specs, out_specs=out_specs, check_vma=False
    )
```

time: 79.2 us -> 61.1 us (0.77)
  Pallas kernels: 0 us -> 13.5 us
  waiting for transfers between devices: 20.5 us -> 7.92 us
  matrix products: 10.3 us -> 0 us
  other arithmetic: 5.65 us -> 0.03 us
  local copies, waits for them, and re-layouts: 14.2 us -> 11.3 us
    pallas_call x0 -> x2, Pallas kernels: none -> 13.5 us  [the longest x1 7.69 us: attention(): pl.pallas_call(attention_kernel, out_shape=jax.ShapeDtypeStruct((288, D),...]
    ppermute x4, waiting for transfers between devices: 20.5 us -> 7.92 us  [shifted(): return lax.ppermute(value, axis, pairs)]
    dot_general x5 -> x0, matrix products: 10.3 us -> none  [the longest x1 3.81 us: expand_tokens(): jnp.dot(coarse.reshape(-1, channels), expand_weight, preferred_element_ty...]
    dot_general x1 -> x0, local copies, waits for them, and re-layouts: 6.54 us -> none  [expand_tokens(): jnp.dot(coarse.reshape(-1, channels), expand_weight, preferred_element_ty...]
    reshape x4 -> x5, local copies, waits for them, and re-layouts: 3.41 us -> 7.61 us  [the longest x1 2.22 us: per_device(): return jnp.transpose(mixed.reshape(ROWS, COLS, Z, D), (2, 0, 1, 3))]
    mul x1 -> x0, other arithmetic: 1.87 us -> none  [window_attention(): key_rows * lax.rsqrt(jnp.sum(key_rows * key_rows, axis=-1, keepdims=True)...]
    slice x4, local copies, waits for them, and re-layouts: 0.1 us -> 1.88 us  [the longest x1 1.01 us: per_device(): right = shifted(own[:HALF], 'lon', -1, True)]
    slice x2 -> x0, other arithmetic: 1.47 us -> none  [the longest x1 1.43 us: window_attention(): packed[2]]
  transfers between devices with their start and end apart: 4 -> 4, of which waited for: 4 -> 3; matrix products, arithmetic and copies ran while one was open for 0% -> 3% of each run, Pallas kernels for 0% -> 0%
where the time goes in v1:
time: 61.1 us; the launch traced here: 60.6 us
  starting transfers between devices  27.7 us (45%)
  Pallas kernels  13.5 us (22%)
  local copies, waits for them, and re-layouts  11.3 us (18%)
  waiting for transfers between devices  7.92 us (13%)
    ppermute x4, starting transfers between devices, shifted(): return lax.ppermute(value, axis, pairs)  27.7 us
    ppermute x4, waiting for transfers between devices, shifted(): return lax.ppermute(value, axis, pairs)  7.92 us
    pallas_call x1, Pallas kernels, attention(): pl.pallas_call(attention_kernel, out_shape=jax.ShapeDtypeStruct((288, D),...  7.69 us
    pallas_call x1, Pallas kernels, expand(): pl.pallas_call(expand_kernel, grid=(4,), out_shape=jax.ShapeDtypeStruct((...  5.83 us
    reshape x1, local copies, waits for them, and re-layouts, per_device(): return jnp.transpose(mixed.reshape(ROWS, COLS, Z, D), (2, 0, 1, 3))  2.22 us
    reshape x1, local copies, waits for them, and re-layouts, expand(): beside = jnp.transpose(skip, (1, 2, 0, 3)).reshape(288, D)  1.8 us
    reshape x1, local copies, waits for them, and re-layouts, expand(): rows = jnp.transpose(coarse, (1, 2, 0, 3)).reshape(72, 1024)  1.63 us
  transfers between devices with their start and end apart: 4, of which 3 were waited for; matrix products, arithmetic and copies ran while one was open for 3% of the time, Pallas kernels for 0%

profile of v1, /device:TPU:4, one launch (start us, length us, event | category | flops | bytes accessed | tf_op | source)
XLA Modules:
  0.0 60.6 jit_solution(5086971825911610298)
XLA Ops:
  0.0 0.8 %reshape.25 = s32[6,2,6,2]{3,2,1,0:T(8,128)S(1)} reshape(s32[12,12]{1,0:T(8,128)} %param.16) | data formatting | bytes 1152 | tf_op jit(solution)/shard_map/reshape | solution.py:95
  0.8 0.2 copy.15
  0.9 0.1 broadcast_in_dim.10
  1.0 0.1 copy.16
  1.2 1.2 %copy.17.surface = s32[4,72,1]{2,1,0:T(8,128)} copy(s32[4,72,1]{0,1,2:T(8,128)S(1)} %bitcast.10) | data formatting | bytes 2304 | tf_op jit(solution)/shard_map/reshape | solution.py:96
  2.4 1.6 %reshape.23.coarse = bf16[72,1024]{1,0:T(8,128)(2,1)} reshape(bf16[6,6,2,1024]{3,2,1,0:T(2,128)(2,1)} %bitcast.9) | data formatting | bytes 294912 | tf_op jit(solution)/shard_map/reshape | solution.py:93
  4.0 1.8 %reshape.24.skip = bf16[288,512]{1,0:T(8,128)(2,1)} reshape(bf16[12,12,2,512]{3,2,1,0:T(2,128)(2,1)} %bitcast.7) | data formatting | bytes 589824 | tf_op jit(solution)/shard_map/reshape | solution.py:94
  5.8 5.8 %expand.1.own = bf16[304,512]{1,0:T(8,128)(2,1)} custom-call(bf16[72,1024]{1,0:T(8,128)(2,1)} %reshape.23.coarse, bf16[1024,2048]{1,0:T(8,128)(2,1)} %weight.2, bf16[288,512]{1,0:T(8,128)(2,1)} %reshape.24.skip, s32[4,72,1]{2,1,0:T(8,128)} %copy.17.surface, f32[3,512]{1,0:T(4,128)} %table.1, f32[1,512]{1,0:T(1,128)} %bitcast.11, ...), custom_call_target="tpu_custom_call" | custom-call | flops 301989888 | bytes 5242880 | tf_op jit(solution)/shard_map/expand/pallas_call | solution.py:98
  11.6 1.0 %fusion.1 = (bf16[152,512]{1,0:T(8,128)(2,1)S(1)}, bf16[152,512]{1,0:T(8,128)(2,1)S(1)}) fusion(bf16[304,512]{1,0:T(8,128)(2,1)} %expand.1.own), kind=kLoop, calls=%fused_computation.3 | loop fusion | bytes 622592 | tf_op jit(solution)/shard_map/slice | solution.py:241
  12.6 5.5 %collective-permute-start.1 = (bf16[152,512]{1,0:T(8,128)(2,1)S(1)}, bf16[152,512]{1,0:T(8,128)(2,1)S(1)}, u32[]{:S(2)}, u32[]{:S(2)}) collective-permute-start(bf16[152,512]{1,0:T(8,128)(2,1)S(1)} %get-tuple-element.9), channel_id=1, source_target_pairs={{0,31},{1,0},{2,1},{3,2},{4,3},{5,4},{6,5},{7,6},{8,7},{9,8},{10,9... | collective-permute-start | bytes 466952 | tf_op jit(solution)/shard_map/ppermute | solution.py:225
  18.1 1.9 %collective-permute-start = (bf16[152,512]{1,0:T(8,128)(2,1)S(1)}, bf16[152,512]{1,0:T(8,128)(2,1)S(1)}, u32[]{:S(2)}, u32[]{:S(2)}) collective-permute-start(bf16[152,512]{1,0:T(8,128)(2,1)S(1)} %get-tuple-element.10), channel_id=1, source_target_pairs={{0,1},{1,2},{2,3},{3,4},{4,5},{5,6},{6,7},{7,8},{8,9},{9,10},{10,1... | collective-permute-start | bytes 466952 | tf_op jit(solution)/shard_map/ppermute | solution.py:225
  20.0 0.9 %fusion = (bf16[40,512]{1,0:T(8,128)(2,1)S(1)}, bf16[40,512]{1,0:T(8,128)(2,1)S(1)}, bf16[40,512]{1,0:T(8,128)(2,1)S(1)}, bf16[40,512]{1,0:T(8,128)(2,1)S(1)}) fusion(bf16[304,512]{1,0:T(8,128)(2,1)} %expand.1.own), kind=kLoop, calls=%fused_computation.2 | loop fusion | bytes 327680 | tf_op jit(solution)/shard_map/slice | solution.py:244
  20.9 0.0 collective-permute-done.1.right
  20.9 5.8 %collective-permute-done.left = bf16[152,512]{1,0:T(8,128)(2,1)S(1)} collective-permute-done((bf16[152,512]{1,0:T(8,128)(2,1)S(1)}, bf16[152,512]{1,0:T(8,128)(2,1)S(1)}, u32[]{:S(2)}, u32[]{:S(2)}) %collective-permute-start) | collective-permute-done | bytes 155680 | tf_op jit(solution)/shard_map/ppermute | solution.py:225
  26.8 4.3 %collective-permute-start.2 = (bf16[160,512]{1,0:T(8,128)(2,1)S(1)}, bf16[160,512]{1,0:T(8,128)(2,1)S(1)}, u32[]{:S(2)}, u32[]{:S(2)}) collective-permute-start(bf16[160,512]{1,0:T(8,128)(2,1)S(1)} %pad_maximum_fusion), channel_id=1, source_target_pairs={{0,32},{32,64},{64,96},{96,128},{128,160},{160,192},{192,224},{224... | collective-permute-start | bytes 491528 | tf_op jit(solution)/shard_map/ppermute | solution.py:225
  31.1 16.1 %collective-permute-start.3 = (bf16[160,512]{1,0:T(8,128)(2,1)S(1)}, bf16[160,512]{1,0:T(8,128)(2,1)S(1)}, u32[]{:S(2)}, u32[]{:S(2)}) collective-permute-start(bf16[160,512]{1,0:T(8,128)(2,1)S(1)} %pad_maximum_fusion.1), channel_id=1, source_target_pairs={{32,0},{64,32},{96,64},{128,96},{160,128},{192,160},{224,192},{256... | collective-permute-start | bytes 491528 | tf_op jit(solution)/shard_map/ppermute | solution.py:225
  47.2 0.1 broadcast_in_dim.12
  47.3 0.7 %reshape_reshape.3.scale = f32[1,512]{1,0:T(1,128)} reshape(f32[8,64]{1,0:T(8,128)S(1)} %broadcast_in_dim.12) | data formatting | bytes 4096 | tf_op jit(solution)/shard_map/reshape;reshape | solution.py:215
  47.9 0.6 collective-permute-done.2.above
  48.5 1.5 %collective-permute-done.3.below = bf16[160,512]{1,0:T(8,128)(2,1)S(1)} collective-permute-done((bf16[160,512]{1,0:T(8,128)(2,1)S(1)}, bf16[160,512]{1,0:T(8,128)(2,1)S(1)}, u32[]{:S(2)}, u32[]{:S(2)}) %collective-permute-start.3) | collective-permute-done | bytes 163872 | tf_op jit(solution)/shard_map/ppermute | solution.py:225
  50.0 0.0 copy-done.1
  50.0 0.7 %copy-done.4 = bf16[160,512]{1,0:T(8,128)(2,1)} copy-done((bf16[160,512]{1,0:T(8,128)(2,1)}, bf16[160,512]{1,0:T(8,128)(2,1)S(1)}, u32[]{:S(2)}) %copy-start.4) | copy-done | bytes 163864
  50.7 7.7 %attention.1 = f32[288,512]{1,0:T(8,128)} custom-call(bf16[304,512]{1,0:T(8,128)(2,1)} %expand.1.own, bf16[152,512]{1,0:T(8,128)(2,1)} %copy-done.1, bf16[152,512]{1,0:T(8,128)(2,1)} %copy-done, bf16[160,512]{1,0:T(8,128)(2,1)} %copy-done.3, bf16[160,512]{1,0:T(8,128)(2,1)} %copy-done.4, f32[1,512]{1,0:T(1,128)} %bitcast.12, bf16[512,1536]{1,0:T(8,128)(2,1)} %weight.3, ...), custom_call_target="tpu_custom_call" | custom-call | flops 4294967296 | bytes 4194304 | tf_op jit(solution)/shard_map/attention/pallas_call | solution.py:199
  58.4 2.2 %reshape.29 = f32[12,12,2,512]{3,2,1,0:T(2,128)} reshape(f32[288,512]{1,0:T(8,128)} %attention.1) | data formatting | bytes 1179648 | tf_op jit(solution)/shard_map/reshape | solution.py:249
  (13 shorter events, 0.1 us)
Async XLA Ops:
  2.4 44.8 %copy-start.2 = (f32[8]{0:T(128)S(1)}, f32[8]{0:T(128)}, u32[]{:S(2)}) copy-start(f32[8]{0:T(128)} %param.22) | copy-start | bytes 100
  12.6 8.2 %collective-permute-start.1 = (bf16[152,512]{1,0:T(8,128)(2,1)S(1)}, bf16[152,512]{1,0:T(8,128)(2,1)S(1)}, u32[]{:S(2)}, u32[]{:S(2)}) collective-permute-start(bf16[152,512]{1,0:T(8,128)(2,1)S(1)} %get-tuple-element.9), channel_id=1, source_target_pairs={{0,31},{1,0},{2,1},{3,2},{4,3},{5,4},{6,5},{7,6},{8,7},{9,8},{10,9... | collective-permute-start | bytes 466952 | tf_op jit(solution)/shard_map/ppermute | solution.py:225
  18.1 8.7 %collective-permute-start = (bf16[152,512]{1,0:T(8,128)(2,1)S(1)}, bf16[152,512]{1,0:T(8,128)(2,1)S(1)}, u32[]{:S(2)}, u32[]{:S(2)}) collective-permute-start(bf16[152,512]{1,0:T(8,128)(2,1)S(1)} %get-tuple-element.10), channel_id=1, source_target_pairs={{0,1},{1,2},{2,3},{3,4},{4,5},{5,6},{6,7},{7,8},{8,9},{9,10},{10,1... | collective-permute-start | bytes 466952 | tf_op jit(solution)/shard_map/ppermute | solution.py:225
  20.9 29.1 %copy-start = (bf16[152,512]{1,0:T(8,128)(2,1)}, bf16[152,512]{1,0:T(8,128)(2,1)S(1)}, u32[]{:S(2)}) copy-start(bf16[152,512]{1,0:T(8,128)(2,1)S(1)} %collective-permute-done.1.right) | copy-start | bytes 466948
  26.8 23.3 %copy-start.1 = (bf16[152,512]{1,0:T(8,128)(2,1)}, bf16[152,512]{1,0:T(8,128)(2,1)S(1)}, u32[]{:S(2)}) copy-start(bf16[152,512]{1,0:T(8,128)(2,1)S(1)} %collective-permute-done.left) | copy-start | bytes 466948
  26.8 21.7 %collective-permute-start.2 = (bf16[160,512]{1,0:T(8,128)(2,1)S(1)}, bf16[160,512]{1,0:T(8,128)(2,1)S(1)}, u32[]{:S(2)}, u32[]{:S(2)}) collective-permute-start(bf16[160,512]{1,0:T(8,128)(2,1)S(1)} %pad_maximum_fusion), channel_id=1, source_target_pairs={{0,32},{32,64},{64,96},{96,128},{128,160},{160,192},{192,224},{224... | collective-permute-start | bytes 491528 | tf_op jit(solution)/shard_map/ppermute | solution.py:225
  31.1 18.9 %collective-permute-start.3 = (bf16[160,512]{1,0:T(8,128)(2,1)S(1)}, bf16[160,512]{1,0:T(8,128)(2,1)S(1)}, u32[]{:S(2)}, u32[]{:S(2)}) collective-permute-start(bf16[160,512]{1,0:T(8,128)(2,1)S(1)} %pad_maximum_fusion.1), channel_id=1, source_target_pairs={{32,0},{64,32},{96,64},{128,96},{160,128},{192,160},{224,192},{256... | collective-permute-start | bytes 491528 | tf_op jit(solution)/shard_map/ppermute | solution.py:225
  48.5 1.5 %copy-start.3 = (bf16[160,512]{1,0:T(8,128)(2,1)}, bf16[160,512]{1,0:T(8,128)(2,1)S(1)}, u32[]{:S(2)}) copy-start(bf16[160,512]{1,0:T(8,128)(2,1)S(1)} %collective-permute-done.2.above) | copy-start | bytes 491524
  50.0 0.7 %copy-start.4 = (bf16[160,512]{1,0:T(8,128)(2,1)}, bf16[160,512]{1,0:T(8,128)(2,1)S(1)}, u32[]{:S(2)}) copy-start(bf16[160,512]{1,0:T(8,128)(2,1)S(1)} %collective-permute-done.3.below) | copy-start | bytes 491524

commit v2 on v0

v2 whole, which is shorter than its diff:
```python
import jax
import jax.numpy as jnp
from jax import lax
from jax.experimental import pallas as pl
from jax.experimental.pallas import tpu as pltpu
from jax.sharding import PartitionSpec as P

D = 512
CD = 1024
HEAD = 64
ROWS = 12
COLS = 12
HALF = 6
EDGE = 3
Z = 2
EPSILON = 1e-05
MIB = 1 << 20


def half_start(half, position):
    return HALF * ((half + position + 1) % 2)


def edge_start(edge, position):
    return (ROWS - EDGE) * ((edge + position + 1) % 2)


def flat(tokens):
    return tokens.reshape(-1, tokens.shape[-1])


def normalized(values, gain):
    average = jnp.mean(values, axis=-1, keepdims=True)
    centred = values - average
    spread = jnp.mean(centred * centred, axis=-1, keepdims=True)
    return centred * lax.rsqrt(spread + EPSILON) * gain


def dot(a, b):
    return jnp.dot(a, b, preferred_element_type=jnp.float32)


def expand_kernel(coarse, weight, skip, surface, table, gain, half0, half1, *scratch):
    even = lax.rem(lax.axis_index("lon"), 2) == 0
    buffer, coarse_in, skip_in, surface_in, table_in, gain_in, arrived = scratch
    small = [
        pltpu.make_async_copy(source, target, arrived.at[4 + at])
        for at, (source, target) in enumerate(
            ((coarse, coarse_in), (surface, surface_in), (table, table_in), (gain, gain_in), (skip, skip_in))
        )
    ]
    large = [
        pltpu.make_async_copy(weight.at[:, phase * D : (phase + 1) * D], buffer.at[phase], arrived.at[phase])
        for phase in range(4)
    ]
    for copy in small + large:
        copy.start()
    place = lax.broadcasted_iota(jnp.int32, (72, ROWS), 0)
    lane = lax.broadcasted_iota(jnp.int32, (72, ROWS), 1)
    for copy in small:
        copy.wait()
    rows = flat(coarse_in[...])
    kinds = surface_in[...].astype(jnp.float32)
    added = []
    for phase in range(4):
        a, b = phase // 2, phase % 2
        row_is = (2 * (place // 12) + a == lane).astype(jnp.float32)
        column_is = 2 * (lax.rem(place, 12) // 2) + b == lane
        kind = jnp.sum(jnp.where(column_is, dot(row_is, kinds), 0.0), axis=-1, keepdims=True)
        term = jnp.where(kind == 0, table_in[0:1], jnp.where(kind == 1, table_in[1:2], table_in[2:3]))
        added.append(flat(skip_in[:, a, :, b]).astype(jnp.float32) + term)
    for phase in range(4):
        a, b = phase // 2, phase % 2
        large[phase].wait()
        fine = normalized(dot(rows, buffer[phase]), gain_in[...])
        made = (added[phase] + fine).reshape(6, 6, Z, D)
        first, second = made[:, :3], made[:, 3:]
        half0[:, a, :, b] = jnp.where(even, second, first).astype(jnp.bfloat16)
        half1[:, a, :, b] = jnp.where(even, first, second).astype(jnp.bfloat16)


VMEM = pl.BlockSpec(memory_space=pltpu.VMEM)
HBM = pl.BlockSpec(memory_space=pltpu.HBM)
SMEM = pl.BlockSpec(memory_space=pltpu.SMEM)


def expand(coarse, skip, land_sea, surf_table, expand_weight, expand_gain):
    half = jax.ShapeDtypeStruct((6, 2, 3, 2, Z, D), jnp.bfloat16)
    halves = pl.pallas_call(
        expand_kernel,
        out_shape=(half, half),
        in_specs=[HBM] * 6,
        out_specs=(VMEM, VMEM),
        scratch_shapes=[
            pltpu.VMEM((4, CD, D), jnp.bfloat16),
            pltpu.VMEM((6, 6, Z, CD), jnp.bfloat16),
            pltpu.VMEM((6, 2, 6, 2, Z, D), jnp.bfloat16),
            pltpu.VMEM((ROWS, COLS), jnp.int32),
            pltpu.VMEM((3, D), jnp.float32),
            pltpu.VMEM((1, D), jnp.float32),
            pltpu.SemaphoreType.DMA((9,)),
        ],
        compiler_params=pltpu.CompilerParams(vmem_limit_bytes=16 * MIB),
        cost_estimate=pl.CostEstimate(flops=2 * 72 * CD * 2048, bytes_accessed=5 * MIB, transcendentals=0),
        name="expand",
    )(
        *(
            pltpu.with_memory_space_constraint(operand, pltpu.HBM)
            for operand in (
                jnp.transpose(coarse, (1, 2, 0, 3)),
                expand_weight,
                jnp.transpose(skip, (1, 2, 0, 3)).reshape(6, 2, 6, 2, Z, D),
                land_sea,
                surf_table,
                expand_gain.reshape(1, D),
            )
        )
    )
    return [part.reshape(ROWS, HALF, Z, D) for part in halves]


def bf16(values):
    return values.astype(jnp.bfloat16)


def head_lanes():
    return lax.broadcasted_iota(jnp.int32, (1, 256), 1) // HEAD


def head_ones():
    return bf16((lax.broadcasted_iota(jnp.int32, (256, 256), 0) // HEAD == head_lanes()).astype(jnp.float32))


def projected(rows, weight, column):
    return bf16(dot(rows, weight[:, column : column + 256]))


def unit(rows, weight, column, ones):
    product = projected(rows, weight, column).astype(jnp.float32)
    squares = dot(bf16(product * product), ones)
    return product * lax.rsqrt(squares + 1e-06)


def scaled_queries(rows, weight, group, scale, ones):
    lane = head_lanes()
    factor = jnp.full((1, 256), scale[4 * group], jnp.float32)
    for h in range(1, 4):
        factor = jnp.where(lane == h, scale[4 * group + h], factor)
    return unit(rows, weight, 256 * group, ones) * factor


def attended(q, keys, values, live=None):
    size = q.shape[0]
    lane = head_lanes()
    stacked = bf16(jnp.concatenate([jnp.where(lane == h, q, 0.0) for h in range(4)], axis=0))
    scores = lax.dot_general(stacked, keys, (((1,), (1,)), ((), ())), preferred_element_type=jnp.float32)
    powers = jnp.exp(scores)
    if live is not None:
        powers = jnp.where(live, powers, 0.0)
    share = 1.0 / jnp.sum(powers, axis=-1, keepdims=True)
    mixed = dot(bf16(powers), values) * share
    result = jnp.where(lane == 0, mixed[:size], 0.0)
    for h in range(1, 4):
        result = jnp.where(lane == h, mixed[h * size : (h + 1) * size], result)
    return bf16(result)


def pairs_of(tokens):
    return tokens.reshape(-1, Z, D)


def middle_kernel(mine0, mine1, beside0, beside1, gain, weight, scale, out_weight, out, made, blended, sent):
    lon = lax.axis_index("lon")
    middle = pl.ds(EDGE, ROWS - 2 * EDGE)
    ones = head_ones()
    tokens = [
        flat(jnp.concatenate([pairs_of(mine[middle]), pairs_of(beside[middle])], axis=0)).astype(jnp.float32)
        for mine, beside in ((mine0, beside0), (mine1, beside1))
    ]
    normed = [normalized(window, gain[...]) for window in tokens]
    every = bf16(jnp.concatenate(normed, axis=0))
    asking = bf16(jnp.concatenate([window[:72] for window in normed], axis=0))
    for group in (0, 1):
        queries = scaled_queries(asking, weight, group, scale, ones)
        keys = bf16(unit(every, weight, D + 256 * group, ones))
        values = projected(every, weight, 2 * D + 256 * group)
        for half in (0, 1):
            window = slice(144 * half, 144 * half + 144)
            blended[72 * half : 72 * half + 72, 256 * group : 256 * group + 256] = attended(
                queries[72 * half : 72 * half + 72], keys[window], values[window]
            )
    result = jnp.concatenate([window[:72] for window in tokens], axis=0) + dot(blended[...], out_weight[...])
    for half in (0, 1):
        made[:, pl.ds(half_start(half, lon), HALF)] = result[72 * half : 72 * half + 72].reshape(6, HALF, Z, D)
    copy = pltpu.make_async_copy(made, out.at[middle], sent)
    copy.start()
    copy.wait()


def edge_kernel(
    mine0, mine1, beside0, beside1, over0, over1, gain, weight, scale, out_weight, begun, out, made, blended, sent
):
    lat, lon = lax.axis_index("lat"), lax.axis_index("lon")
    last = lax.axis_size("lat") - 1
    ones = head_ones()
    tokens = []
    for edge, over in ((0, over0), (1, over1)):
        rows = pl.ds(edge_start(edge, lat), EDGE)
        for half, mine, beside in ((0, mine0, beside0), (1, mine1, beside1)):
            window = [mine[rows], beside[rows], over[2 * half], over[2 * half + 1]]
            window = jnp.concatenate([pairs_of(w) for w in window], axis=0)
            tokens.append(flat(window).astype(jnp.float32))
    normed = [normalized(window, gain[...]) for window in tokens]
    every = bf16(jnp.concatenate(normed, axis=0))
    asking = bf16(jnp.concatenate([window[:40] for window in normed], axis=0))
    paired = jnp.where((lat > 0) & (lat < last), 144, 72)
    live = lax.broadcasted_iota(jnp.int32, (1, 144), 1) < paired
    for group in (0, 1):
        queries = scaled_queries(asking, weight, group, scale, ones)
        keys = bf16(unit(every, weight, D + 256 * group, ones))
        values = projected(every, weight, 2 * D + 256 * group)
        for at in range(4):
            window = slice(144 * at, 144 * at + 144)
            blended[40 * at : 40 * at + 40, 256 * group : 256 * group + 256] = attended(
                queries[40 * at : 40 * at + 40], keys[window], values[window], live if at >= 2 else None
            ).astype(jnp.float32)
    result = jnp.concatenate([window[:40] for window in tokens], axis=0) + dot(bf16(blended[...]), out_weight[...])
    copies = []
    for edge in (0, 1):
        for half in (0, 1):
            at = 40 * (2 * edge + half)
            part = result[at : at + 40].reshape(20, Z, D)[:18].reshape(EDGE, HALF, Z, D)
            made[edge, :, pl.ds(half_start(half, lon), HALF)] = part
        rows = pl.ds(edge_start(edge, lat), EDGE)
        copies.append(pltpu.make_async_copy(made.at[edge], out.at[rows], sent.at[edge]))
    for copy in copies:
        copy.start()
    for copy in copies:
        copy.wait()


OUT = jax.ShapeDtypeStruct((ROWS, COLS, Z, D), jnp.float32)


def middle_windows(mine, beside, parameters):
    return pl.pallas_call(
        middle_kernel,
        out_shape=OUT,
        in_specs=[VMEM] * 6 + [SMEM, VMEM],
        out_specs=HBM,
        scratch_shapes=[
            pltpu.VMEM((6, COLS, Z, D), jnp.float32),
            pltpu.VMEM((144, D), jnp.bfloat16),
            pltpu.SemaphoreType.DMA(()),
        ],
        compiler_params=pltpu.CompilerParams(vmem_limit_bytes=32 * MIB),
        cost_estimate=pl.CostEstimate(flops=2 << 30, bytes_accessed=2 * MIB, transcendentals=350000),
        name="middle",
    )(*mine, *beside, *parameters)


def edge_windows(mine, beside, over, parameters, begun):
    return pl.pallas_call(
        edge_kernel,
        out_shape=OUT,
        in_specs=[VMEM] * 8 + [SMEM, VMEM, HBM],
        out_specs=HBM,
        scratch_shapes=[
            pltpu.VMEM((2, EDGE, COLS, Z, D), jnp.float32),
            pltpu.VMEM((160, D), jnp.float32),
            pltpu.SemaphoreType.DMA((2,)),
        ],
        input_output_aliases={10: 0},
        compiler_params=pltpu.CompilerParams(vmem_limit_bytes=32 * MIB),
        cost_estimate=pl.CostEstimate(flops=2 << 30, bytes_accessed=2 * MIB, transcendentals=350000),
        name="edges",
    )(*mine, *beside, *over, *parameters, begun)


def swapped(value, axis, turn, ring):
    count = lax.axis_size(axis)
    pairs = []
    for source in range(count):
        target = source + 1 if source % 2 == turn else source - 1
        if not ring and not 0 <= target < count:
            target = source
        pairs.append((source, target % count))
    return lax.ppermute(value, axis, pairs)


def per_device(
    coarse,
    skip_tokens,
    land_sea,
    surf_table,
    expand_weight,
    expand_gain,
    attn_gain,
    qkv_weight,
    logit_scale,
    out_weight,
):
    mine = expand(coarse, skip_tokens, land_sea, surf_table, expand_weight, expand_gain)
    beside = [swapped(mine[turn], "lon", turn, True) for turn in (0, 1)]
    lat = lax.axis_index("lat")
    over = [None, None]
    for turn in (1, 0):
        parts = [
            lax.dynamic_slice_in_dim(part, edge_start(turn, lat), EDGE, 0)
            for part in (mine[0], beside[0], mine[1], beside[1])
        ]
        over[turn] = swapped(jnp.stack(parts), "lat", turn, False)
    parameters = (attn_gain.reshape(1, D), qkv_weight, logit_scale, out_weight)
    begun = middle_windows(mine, beside, parameters)
    mixed = edge_windows(mine, beside, over, parameters, begun)
    return jnp.transpose(mixed, (2, 0, 1, 3))


def solution(mesh):
    in_specs = (
        P(None, "lat", "lon", None),
        P(None, "lat", "lon", None),
        P("lat", "lon"),
        P(),
        P(),
        P(),
        P(),
        P(),
        P(),
        P(),
    )
    out_specs = P(None, "lat", "lon", None)
    return jax.shard_map(
        per_device, mesh=mesh, in_specs=in_specs, out_specs=out_specs, check_vma=False
    )
```

time: 79.2 us -> 43.1 us (0.54)
  the two profiles are of different devices: /device:TPU:4 before, /device:TPU:31 now
where the time goes in v2:
time: 43.1 us; the launch traced here: 42.9 us
  starting transfers between devices  28.1 us (65%)
  Pallas kernels  11.6 us (27%)
  waiting for transfers between devices  2.17 us (5%)
  other arithmetic  0.53 us (1%)
    ppermute x4, starting transfers between devices, swapped(): return lax.ppermute(value, axis, pairs)  28.1 us
    pallas_call x1, Pallas kernels, edge_windows(): pl.pallas_call(edge_kernel, out_shape=OUT, in_specs=[VMEM] * 8 + [SMEM, V...  4.59 us
    pallas_call x1, Pallas kernels, expand(): pl.pallas_call(expand_kernel, out_shape=(half, half), in_specs=[HBM] * 6,...  3.82 us
    pallas_call x1, Pallas kernels, middle_windows(): pl.pallas_call(middle_kernel, out_shape=OUT, in_specs=[VMEM] * 6 + [SMEM,...  3.22 us
    ppermute x4, waiting for transfers between devices, swapped(): return lax.ppermute(value, axis, pairs)  2.17 us
  transfers between devices with their start and end apart: 4, of which 2 were waited for; matrix products, arithmetic and copies ran while one was open for 1% of the time, Pallas kernels for 8%

profile of v2, /device:TPU:31, one launch (start us, length us, event | category | flops | bytes accessed | tf_op | source)
XLA Modules:
  0.0 42.9 jit_solution(11259620060878254834)
XLA Ops:
  0.0 0.0 copy-start.1
  0.0 0.0 copy-start.3
  0.0 0.0 copy-start
  0.0 0.0 copy-start.2
  0.0 3.8 %expand.1 = (bf16[6,2,3,2,2,512]{5,4,3,2,1,0:T(2,128)(2,1)S(1)}, bf16[6,2,3,2,2,512]{5,4,3,2,1,0:T(2,128)(2,1)S(1)}) custom-call(bf16[6,6,2,1024]{3,2,1,0:T(2,128)(2,1)} %bitcast.36, bf16[1024,2048]{1,0:T(8,128)(2,1)} %weight.3, bf16[6,2,6,2,2,512]{5,4,3,2,1,0:T(2,128)(2,1)} %bitcast.35, s32[12,12]{1,0:T(8,128)} %surface.1, f32[3,512]{1,0:T(4,128)} %table.1, ...), custom_call_target="tpu_custom_call" | custom-call | flops 301989888 | bytes 5242880 | tf_op jit(solution)/shard_map/expand/pallas_call | solution.py:89
  3.8 5.2 %collective-permute-start.1 = (bf16[12,6,2,512]{3,2,1,0:T(2,128)(2,1)S(1)}, bf16[12,6,2,512]{3,2,1,0:T(2,128)(2,1)S(1)}, u32[]{:S(2)}, u32[]{:S(2)}) collective-permute-start(bf16[12,6,2,512]{3,2,1,0:T(2,128)(2,1)S(1)} %bitcast.29), channel_id=1, source_target_pairs={{0,31},{1,2},{2,1},{3,4},{4,3},{5,6},{6,5},{7,8},{8,7},{9,10},{10,... | collective-permute-start | bytes 442376 | tf_op jit(solution)/shard_map/ppermute | solution.py:288
  9.1 1.9 %collective-permute-start = (bf16[12,6,2,512]{3,2,1,0:T(2,128)(2,1)S(1)}, bf16[12,6,2,512]{3,2,1,0:T(2,128)(2,1)S(1)}, u32[]{:S(2)}, u32[]{:S(2)}) collective-permute-start(bf16[12,6,2,512]{3,2,1,0:T(2,128)(2,1)S(1)} %bitcast.25), channel_id=1, source_target_pairs={{0,1},{1,0},{2,3},{3,2},{4,5},{5,4},{6,7},{7,6},{8,9},{9,8},{10,11... | collective-permute-start | bytes 442376 | tf_op jit(solution)/shard_map/ppermute | solution.py:288
  11.1 0.1 dynamic-slice_bitcast_fusion.1
  11.2 1.2 %collective-permute-done.1.beside1 = bf16[12,6,2,512]{3,2,1,0:T(2,128)(2,1)S(1)} collective-permute-done((bf16[12,6,2,512]{3,2,1,0:T(2,128)(2,1)S(1)}, bf16[12,6,2,512]{3,2,1,0:T(2,128)(2,1)S(1)}, u32[]{:S(2)}, u32[]{:S(2)}) %collective-permute-start.1) | collective-permute-done | bytes 147488 | tf_op jit(solution)/shard_map/ppermute | solution.py:288
  12.4 0.1 dynamic-slice_bitcast_fusion
  12.5 0.0 collective-permute-done.beside0
  12.5 0.1 dynamic-slice_bitcast_fusion.2
  12.6 0.3 pad_maximum_fusion
  12.8 4.0 %collective-permute-start.2 = (bf16[4,3,6,2,512]{4,3,2,1,0:T(2,128)(2,1)S(1)}, bf16[4,3,6,2,512]{4,3,2,1,0:T(2,128)(2,1)S(1)}, u32[]{:S(2)}, u32[]{:S(2)}) collective-permute-start(bf16[4,3,6,2,512]{4,3,2,1,0:T(2,128)(2,1)S(1)} %pad_maximum_fusion), channel_id=1, source_target_pairs={{0,32},{32,0},{64,96},{96,64},{128,160},{160,128},{192,224},{224,1... | collective-permute-start | bytes 442376 | tf_op jit(solution)/shard_map/ppermute | solution.py:288
  16.8 0.3 pad_maximum_fusion.1
  17.1 17.0 %collective-permute-start.3 = (bf16[4,3,6,2,512]{4,3,2,1,0:T(2,128)(2,1)S(1)}, bf16[4,3,6,2,512]{4,3,2,1,0:T(2,128)(2,1)S(1)}, u32[]{:S(2)}, u32[]{:S(2)}) collective-permute-start(bf16[4,3,6,2,512]{4,3,2,1,0:T(2,128)(2,1)S(1)} %pad_maximum_fusion.1), channel_id=1, source_target_pairs={{0,0},{32,64},{64,32},{96,128},{128,96},{160,192},{192,160},{224,2... | collective-permute-start | bytes 442376 | tf_op jit(solution)/shard_map/ppermute | solution.py:288
  34.1 0.0 copy-done.1
  34.1 0.0 copy-done.3
  34.1 0.0 copy-done
  34.1 0.0 copy-done.2
  34.1 3.2 %middle.1.begun = f32[12,12,2,512]{3,2,1,0:T(2,128)} custom-call(bf16[12,6,2,512]{3,2,1,0:T(2,128)(2,1)S(1)} %bitcast.27, bf16[12,6,2,512]{3,2,1,0:T(2,128)(2,1)S(1)} %bitcast.31, bf16[12,6,2,512]{3,2,1,0:T(2,128)(2,1)S(1)} %collective-permute-done.beside0, bf16[12,6,2,512]{3,2,1,0:T(2,128)(2,1)S(1)} %collective-permute-done.1.beside1, ...), custom_call_target="tpu_custom_call" | custom-call | flops 2147483648 | bytes 2097152 | tf_op jit(solution)/shard_map/middle/pallas_call | solution.py:246
  37.4 0.0 collective-permute-done.2.over0
  37.4 0.9 %collective-permute-done.3.over1 = bf16[4,3,6,2,512]{4,3,2,1,0:T(2,128)(2,1)S(1)} collective-permute-done((bf16[4,3,6,2,512]{4,3,2,1,0:T(2,128)(2,1)S(1)}, bf16[4,3,6,2,512]{4,3,2,1,0:T(2,128)(2,1)S(1)}, u32[]{:S(2)}, u32[]{:S(2)}) %collective-permute-start.3) | collective-permute-done | bytes 147488 | tf_op jit(solution)/shard_map/ppermute | solution.py:288
  38.3 4.6 %edges.1 = f32[12,12,2,512]{3,2,1,0:T(2,128)} custom-call(bf16[12,6,2,512]{3,2,1,0:T(2,128)(2,1)S(1)} %bitcast.28, bf16[12,6,2,512]{3,2,1,0:T(2,128)(2,1)S(1)} %bitcast.32, bf16[12,6,2,512]{3,2,1,0:T(2,128)(2,1)S(1)} %collective-permute-done.beside0, bf16[12,6,2,512]{3,2,1,0:T(2,128)(2,1)S(1)} %collective-permute-done.1.beside1, ...), custom_call_target="tpu_custom_call", output_to_operand_aliasing={{}: (10, {})} | custom-call | flops 2147483648 | bytes 2097152 | tf_op jit(solution)/shard_map/edges/pallas_call | solution.py:263
Async XLA Ops:
  0.0 34.1 %copy-start.1 = (bf16[512,512]{1,0:T(8,128)(2,1)S(1)}, bf16[512,512]{1,0:T(8,128)(2,1)}, u32[]{:S(2)}) copy-start(bf16[512,512]{1,0:T(8,128)(2,1)} %out_weight.3) | copy-start | bytes 1572868
  0.0 34.1 %copy-start.3 = (f32[8]{0:T(128)S(1)}, f32[8]{0:T(128)}, u32[]{:S(2)}) copy-start(f32[8]{0:T(128)} %scale.3) | copy-start | bytes 100
  0.0 34.1 %copy-start = (bf16[512,1536]{1,0:T(8,128)(2,1)S(1)}, bf16[512,1536]{1,0:T(8,128)(2,1)}, u32[]{:S(2)}) copy-start(bf16[512,1536]{1,0:T(8,128)(2,1)} %weight.5) | copy-start | bytes 4718596
  0.0 34.1 %copy-start.2 = (f32[512]{0:T(512)S(1)}, f32[512]{0:T(512)}, u32[]{:S(2)}) copy-start(f32[512]{0:T(512)} %param.16) | copy-start | bytes 6148
  3.8 8.6 %collective-permute-start.1 = (bf16[12,6,2,512]{3,2,1,0:T(2,128)(2,1)S(1)}, bf16[12,6,2,512]{3,2,1,0:T(2,128)(2,1)S(1)}, u32[]{:S(2)}, u32[]{:S(2)}) collective-permute-start(bf16[12,6,2,512]{3,2,1,0:T(2,128)(2,1)S(1)} %bitcast.29), channel_id=1, source_target_pairs={{0,31},{1,2},{2,1},{3,4},{4,3},{5,6},{6,5},{7,8},{8,7},{9,10},{10,... | collective-permute-start | bytes 442376 | tf_op jit(solution)/shard_map/ppermute | solution.py:288
  9.1 3.4 %collective-permute-start = (bf16[12,6,2,512]{3,2,1,0:T(2,128)(2,1)S(1)}, bf16[12,6,2,512]{3,2,1,0:T(2,128)(2,1)S(1)}, u32[]{:S(2)}, u32[]{:S(2)}) collective-permute-start(bf16[12,6,2,512]{3,2,1,0:T(2,128)(2,1)S(1)} %bitcast.25), channel_id=1, source_target_pairs={{0,1},{1,0},{2,3},{3,2},{4,5},{5,4},{6,7},{7,6},{8,9},{9,8},{10,11... | collective-permute-start | bytes 442376 | tf_op jit(solution)/shard_map/ppermute | solution.py:288
  12.8 24.5 %collective-permute-start.2 = (bf16[4,3,6,2,512]{4,3,2,1,0:T(2,128)(2,1)S(1)}, bf16[4,3,6,2,512]{4,3,2,1,0:T(2,128)(2,1)S(1)}, u32[]{:S(2)}, u32[]{:S(2)}) collective-permute-start(bf16[4,3,6,2,512]{4,3,2,1,0:T(2,128)(2,1)S(1)} %pad_maximum_fusion), channel_id=1, source_target_pairs={{0,32},{32,0},{64,96},{96,64},{128,160},{160,128},{192,224},{224,1... | collective-permute-start | bytes 442376 | tf_op jit(solution)/shard_map/ppermute | solution.py:288
  17.1 21.2 %collective-permute-start.3 = (bf16[4,3,6,2,512]{4,3,2,1,0:T(2,128)(2,1)S(1)}, bf16[4,3,6,2,512]{4,3,2,1,0:T(2,128)(2,1)S(1)}, u32[]{:S(2)}, u32[]{:S(2)}) collective-permute-start(bf16[4,3,6,2,512]{4,3,2,1,0:T(2,128)(2,1)S(1)} %pad_maximum_fusion.1), channel_id=1, source_target_pairs={{0,0},{32,64},{64,32},{96,128},{128,96},{160,192},{192,160},{224,2... | collective-permute-start | bytes 442376 | tf_op jit(solution)/shard_map/ppermute | solution.py:288

commit v3 on v2

v3 whole, which is shorter than its diff:
```python
import jax
import jax.numpy as jnp
from jax import lax
from jax.experimental import pallas as pl
from jax.experimental.pallas import tpu as pltpu
from jax.sharding import PartitionSpec as P


D = 512
CD = 1024
HEAD = 64
ROWS = 12
COLS = 12
HALF = 6
EDGE = 3
Z = 2
EPSILON = 1e-05
MIB = 1 << 20


def half_start(half, position):
    return HALF * ((half + position + 1) % 2)


def edge_start(edge, position):
    return (ROWS - EDGE) * ((edge + position + 1) % 2)


def flat(tokens):
    return tokens.reshape(-1, tokens.shape[-1])


def normalized(values, gain):
    average = jnp.mean(values, axis=-1, keepdims=True)
    centred = values - average
    spread = jnp.mean(centred * centred, axis=-1, keepdims=True)
    return centred * lax.rsqrt(spread + EPSILON) * gain


def dot(a, b):
    return jnp.dot(a, b, preferred_element_type=jnp.float32)


def pairs_of(tokens):
    return tokens.reshape(-1, Z, tokens.shape[-1])


def expand_kernel(coarse, weight, skip, surface, table, gain, attn_gain, qkv, *refs):
    position = lax.axis_index("lon")
    tokens, normed, qkv_out = refs[0:2], refs[2:4], refs[4]
    buffer, coarse_in, skip_in, surface_in, table_in, gain_in, attn_gain_in, arrived = refs[5:]
    small = [
        pltpu.make_async_copy(source, target, arrived.at[4 + at])
        for at, (source, target) in enumerate(
            (
                (coarse, coarse_in),
                (surface, surface_in),
                (table, table_in),
                (gain, gain_in),
                (attn_gain, attn_gain_in),
                (skip, skip_in),
            )
        )
    ]
    large = [
        pltpu.make_async_copy(weight.at[:, phase * D : (phase + 1) * D], buffer.at[phase], arrived.at[phase])
        for phase in range(4)
    ]
    later = pltpu.make_async_copy(qkv, qkv_out, arrived.at[10])
    for copy in (*small, *large, later):
        copy.start()
    starts = [half_start(half, position) // 2 for half in (0, 1)]
    place = lax.broadcasted_iota(jnp.int32, (72, ROWS), 0)
    lane = lax.broadcasted_iota(jnp.int32, (72, ROWS), 1)
    inside = lax.rem(place, 36)
    row = 2 * (inside // 6)
    column = 2 * (lax.rem(inside, 6) // 2 + jnp.where(place < 36, starts[0], starts[1]))
    for copy in small:
        copy.wait()

    def by_halves(part):
        return flat(jnp.concatenate([pairs_of(part(pl.ds(start, 3))) for start in starts], axis=0))

    rows = by_halves(lambda columns: coarse_in[:, columns])
    kinds = surface_in[...].astype(jnp.float32)
    added = []
    for phase in range(4):
        a, b = phase // 2, phase % 2
        picked = dot((row + a == lane).astype(jnp.float32), kinds)
        kind = jnp.sum(jnp.where(column + b == lane, picked, 0.0), axis=-1, keepdims=True)
        term = jnp.where(kind == 0, table_in[0:1], jnp.where(kind == 1, table_in[1:2], table_in[2:3]))
        added.append(by_halves(lambda columns: skip_in[:, a, columns, b]).astype(jnp.float32) + term)

    def finish(phase, expanded):
        a, b = phase // 2, phase % 2
        made = (added[phase] + normalized(expanded, gain_in[...])).astype(jnp.bfloat16)
        ready = normalized(made.astype(jnp.float32), attn_gain_in[...]).astype(jnp.bfloat16)
        for values, halves in ((made, tokens), (ready, normed)):
            values = pairs_of(values)
            halves[0][:, a, :, b] = values[:18].reshape(6, 3, Z, D)
            halves[1][:, a, :, b] = values[18:].reshape(6, 3, Z, D)

    waiting = None
    for phase in range(4):
        large[phase].wait()
        expanded = dot(rows, buffer[phase])
        if waiting is not None:
            finish(phase - 1, waiting)
        waiting = expanded
    finish(3, waiting)
    later.wait()


VMEM = pl.BlockSpec(memory_space=pltpu.VMEM)
HBM = pl.BlockSpec(memory_space=pltpu.HBM)
SMEM = pl.BlockSpec(memory_space=pltpu.SMEM)


def expand(coarse, skip, land_sea, surf_table, expand_weight, expand_gain, attn_gain, qkv_weight):
    half = jax.ShapeDtypeStruct((6, 2, 3, 2, Z, D), jnp.bfloat16)
    *halves, qkv_weight = pl.pallas_call(
        expand_kernel,
        out_shape=(half,) * 4 + (jax.ShapeDtypeStruct(qkv_weight.shape, jnp.bfloat16),),
        in_specs=[HBM] * 8,
        out_specs=(VMEM,) * 5,
        scratch_shapes=[
            pltpu.VMEM((4, CD, D), jnp.bfloat16),
            pltpu.VMEM((6, 6, Z, CD), jnp.bfloat16),
            pltpu.VMEM((6, 2, 6, 2, Z, D), jnp.bfloat16),
            pltpu.VMEM((ROWS, COLS), jnp.int32),
            pltpu.VMEM((3, D), jnp.float32),
            pltpu.VMEM((1, D), jnp.float32),
            pltpu.VMEM((1, D), jnp.float32),
            pltpu.SemaphoreType.DMA((11,)),
        ],
        compiler_params=pltpu.CompilerParams(vmem_limit_bytes=16 * MIB),
        cost_estimate=pl.CostEstimate(flops=2 * 72 * CD * 2048, bytes_accessed=5 * MIB, transcendentals=0),
        name="expand",
    )(
        *(
            pltpu.with_memory_space_constraint(operand, pltpu.HBM)
            for operand in (
                jnp.transpose(coarse, (1, 2, 0, 3)),
                expand_weight,
                jnp.transpose(skip, (1, 2, 0, 3)).reshape(6, 2, 6, 2, Z, D),
                land_sea,
                surf_table,
                expand_gain.reshape(1, D),
                attn_gain.reshape(1, D),
                qkv_weight,
            )
        )
    )
    halves = [part.reshape(ROWS, HALF, Z, D) for part in halves]
    return halves[:2], halves[2:], qkv_weight


def bf16(values):
    return values.astype(jnp.bfloat16)


def head_lanes():
    return lax.broadcasted_iota(jnp.int32, (1, 256), 1) // HEAD


def head_ones():
    return bf16((lax.broadcasted_iota(jnp.int32, (256, 256), 0) // HEAD == head_lanes()).astype(jnp.float32))


def projected(rows, weight, column):
    return bf16(dot(rows, weight[:, column : column + 256]))


def unit(rows, weight, column, ones):
    product = projected(rows, weight, column).astype(jnp.float32)
    squares = dot(bf16(product * product), ones)
    return product * lax.rsqrt(squares + 1e-06)


def scaled_queries(rows, weight, group, scale, ones):
    lane = head_lanes()
    factor = jnp.full((1, 256), scale[4 * group], jnp.float32)
    for h in range(1, 4):
        factor = jnp.where(lane == h, scale[4 * group + h], factor)
    return unit(rows, weight, 256 * group, ones) * factor


def attended(q, keys, values, live=None):
    size = q.shape[0]
    lane = head_lanes()
    stacked = bf16(jnp.concatenate([jnp.where(lane == h, q, 0.0) for h in range(4)], axis=0))
    scores = lax.dot_general(stacked, keys, (((1,), (1,)), ((), ())), preferred_element_type=jnp.float32)
    powers = jnp.exp(scores)
    if live is not None:
        powers = jnp.where(live, powers, 0.0)
    share = 1.0 / jnp.sum(powers, axis=-1, keepdims=True)
    mixed = dot(bf16(powers), values) * share
    result = jnp.where(lane == 0, mixed[:size], 0.0)
    for h in range(1, 4):
        result = jnp.where(lane == h, mixed[h * size : (h + 1) * size], result)
    return bf16(result)


def middle_kernel(
    own0, own1, mine0, mine1, beside0, beside1, weight, scale, projection, out, keys, values, queries, out_weight, every, made, blended, sent
):
    lat, lon = lax.axis_index("lat"), lax.axis_index("lon")
    middle = pl.ds(EDGE, ROWS - 2 * EDGE)
    ones = head_ones()
    fetched = pltpu.make_async_copy(projection, out_weight, sent.at[1])
    fetched.start()
    asking = []
    for half, mine, beside in ((0, mine0, beside0), (1, mine1, beside1)):
        every[144 * half : 144 * half + 144] = flat(
            jnp.concatenate([pairs_of(mine[middle]), pairs_of(beside[middle])], axis=0)
        )
        for edge in (0, 1):
            rows = pl.ds(edge_start(edge, lat), EDGE)
            at = 288 + 72 * (2 * edge + half)
            every[at : at + 72] = flat(jnp.concatenate([pairs_of(mine[rows]), pairs_of(beside[rows])], axis=0))
        asking.append(every[144 * half : 144 * half + 72])
    asking += [every[288 + 72 * at : 288 + 72 * at + 40] for at in range(4)]
    asking = bf16(jnp.concatenate([part.astype(jnp.float32) for part in asking], axis=0))
    for group in (0, 1):
        lanes = slice(256 * group, 256 * group + 256)
        query = scaled_queries(asking, weight, group, scale, ones)
        key = unit(every[...], weight, D + 256 * group, ones)
        value = projected(every[...], weight, 2 * D + 256 * group)
        for half in (0, 1):
            window = slice(144 * half, 144 * half + 144)
            blended[72 * half : 72 * half + 72, lanes] = attended(
                query[72 * half : 72 * half + 72], bf16(key[window]), value[window]
            )
        keys[:, lanes] = key[288:]
        values[:, lanes] = value[288:].astype(jnp.float32)
        queries[:, lanes] = query[144:]
    tokens = [flat(own[middle]).astype(jnp.float32) for own in (own0, own1)]
    fetched.wait()
    result = jnp.concatenate(tokens, axis=0) + dot(blended[...], out_weight[...])
    for half in (0, 1):
        made[:, pl.ds(half_start(half, lon), HALF)] = result[72 * half : 72 * half + 72].reshape(6, HALF, Z, D)
    copy = pltpu.make_async_copy(made, out.at[middle], sent.at[0])
    copy.start()
    copy.wait()


def edge_kernel(
    own0, own1, over0, seam0, over1, weight, out_weight, keys, values, queries, begun, out, made, blended, sent
):
    lat, lon = lax.axis_index("lat"), lax.axis_index("lon")
    last = lax.axis_size("lat") - 1
    ones = head_ones()
    received = []
    seam = seam_of("lat")
    at_seam = (lat == seam) | (lat == seam - 1)
    for over in (over0, over1):
        for half in (0, 1):
            part = over[2 * half : 2 * half + 2]
            if over is over0:
                part = jnp.where(at_seam, seam0[2 * half : 2 * half + 2], part)
            received.append(flat(pairs_of(part)))
    received = bf16(jnp.concatenate([part.astype(jnp.float32) for part in received], axis=0))
    paired = jnp.where((lat > 0) & (lat < last), 144, 72)
    live = lax.broadcasted_iota(jnp.int32, (1, 144), 1) < paired
    for group in (0, 1):
        lanes = slice(256 * group, 256 * group + 256)
        key = unit(received, weight, D + 256 * group, ones)
        value = projected(received, weight, 2 * D + 256 * group).astype(jnp.float32)
        for at in range(4):
            far = slice(72 * at, 72 * at + 72)
            blended[40 * at : 40 * at + 40, lanes] = attended(
                queries[40 * at : 40 * at + 40, lanes],
                bf16(jnp.concatenate([keys[far, lanes], key[far]], axis=0)),
                bf16(jnp.concatenate([values[far, lanes], value[far]], axis=0)),
                live if at >= 2 else None,
            ).astype(jnp.float32)
    result = dot(bf16(blended[...]), out_weight[...])
    copies = []
    for edge in (0, 1):
        rows = pl.ds(edge_start(edge, lat), EDGE)
        for half, own in ((0, own0), (1, own1)):
            at = 40 * (2 * edge + half)
            part = result[at : at + 40].reshape(20, Z, D)[:18].reshape(EDGE, HALF, Z, D)
            made[edge, :, pl.ds(half_start(half, lon), HALF)] = own[rows].astype(jnp.float32) + part
        copies.append(pltpu.make_async_copy(made.at[edge], out.at[rows], sent.at[edge]))
    for copy in copies:
        copy.start()
    for copy in copies:
        copy.wait()


OUT = jax.ShapeDtypeStruct((ROWS, COLS, Z, D), jnp.float32)


def middle_windows(own, mine, beside, qkv_weight, logit_scale, out_weight):
    return pl.pallas_call(
        middle_kernel,
        out_shape=(
            OUT,
            jax.ShapeDtypeStruct((288, D), jnp.float32),
            jax.ShapeDtypeStruct((288, D), jnp.float32),
            jax.ShapeDtypeStruct((160, D), jnp.float32),
            jax.ShapeDtypeStruct((D, D), jnp.bfloat16),
        ),
        in_specs=[VMEM] * 7 + [SMEM, HBM],
        out_specs=(HBM, VMEM, VMEM, VMEM, VMEM),
        scratch_shapes=[
            pltpu.VMEM((576, D), jnp.bfloat16),
            pltpu.VMEM((6, COLS, Z, D), jnp.float32),
            pltpu.VMEM((144, D), jnp.bfloat16),
            pltpu.SemaphoreType.DMA((2,)),
        ],
        compiler_params=pltpu.CompilerParams(vmem_limit_bytes=32 * MIB),
        cost_estimate=pl.CostEstimate(flops=2 << 30, bytes_accessed=2 * MIB, transcendentals=350000),
        name="middle",
    )(*own, *mine, *beside, qkv_weight, logit_scale, pltpu.with_memory_space_constraint(out_weight, pltpu.HBM))


def edge_windows(own, over, qkv_weight, begun, keys, values, queries, out_weight):
    return pl.pallas_call(
        edge_kernel,
        out_shape=OUT,
        in_specs=[VMEM] * 10 + [HBM],
        out_specs=HBM,
        scratch_shapes=[
            pltpu.VMEM((2, EDGE, COLS, Z, D), jnp.float32),
            pltpu.VMEM((160, D), jnp.float32),
            pltpu.SemaphoreType.DMA((2,)),
        ],
        input_output_aliases={10: 0},
        compiler_params=pltpu.CompilerParams(vmem_limit_bytes=32 * MIB),
        cost_estimate=pl.CostEstimate(flops=1 << 30, bytes_accessed=2 * MIB, transcendentals=350000),
        name="edges",
    )(*own, *over, qkv_weight, out_weight, keys, values, queries, begun)


def seam_of(axis):
    return lax.axis_size(axis) // 2 - 1


def swapped(value, axis, turn, ring, places=None):
    count = lax.axis_size(axis)
    pairs = []
    for source in range(count) if places is None else places:
        target = source + 1 if source % 2 == turn else source - 1
        if not ring and not 0 <= target < count:
            target = source
        pairs.append((source, target % count))
    return lax.ppermute(value, axis, pairs)


def per_device(
    coarse,
    skip_tokens,
    land_sea,
    surf_table,
    expand_weight,
    expand_gain,
    attn_gain,
    qkv_weight,
    logit_scale,
    out_weight,
):
    own, mine, qkv_weight = expand(
        coarse, skip_tokens, land_sea, surf_table, expand_weight, expand_gain, attn_gain, qkv_weight
    )
    beside = []
    for turn in (0, 1):
        beside.append(swapped(mine[turn], "lon", turn, True))
    lat = lax.axis_index("lat")

    def rows_for(turn):
        return jnp.stack(
            [
                lax.dynamic_slice_in_dim(part, edge_start(turn, lat), EDGE, 0)
                for part in (mine[0], beside[0], mine[1], beside[1])
            ]
        )

    seam = seam_of("lat")
    at_seam = [seam - 1, seam]
    rows = [rows_for(turn) for turn in (0, 1)]
    over0 = swapped(rows[0], "lat", 0, False, [at for at in range(lax.axis_size("lat")) if at not in at_seam])
    over1 = swapped(rows[1], "lat", 1, False)
    seam0 = swapped(rows[0], "lat", 0, False, at_seam)
    over = (over0, seam0, over1)
    begun, *held = middle_windows(own, mine, beside, qkv_weight, logit_scale, out_weight)
    mixed = edge_windows(own, over, qkv_weight, begun, *held)
    return jnp.transpose(mixed, (2, 0, 1, 3))


def solution(mesh):
    in_specs = (
        P(None, "lat", "lon", None),
        P(None, "lat", "lon", None),
        P("lat", "lon"),
        P(),
        P(),
        P(),
        P(),
        P(),
        P(),
        P(),
    )
    out_specs = P(None, "lat", "lon", None)
    return jax.shard_map(
        per_device, mesh=mesh, in_specs=in_specs, out_specs=out_specs, check_vma=False
    )
```

time: 43.1 us -> 43.6 us (1.012)
  Pallas kernels: 11.6 us -> 9.91 us
  waiting for transfers between devices: 2.17 us -> 3.76 us
  starting transfers between devices: 28.1 us -> 28.8 us
    pallas_call x3, Pallas kernels: 11.6 us -> 9.91 us  [the longest x1 4.11 us: middle_windows(): pl.pallas_call(middle_kernel, out_shape=(OUT, jax.ShapeDtypeStruct((288,...]
    ppermute x4 -> x5, waiting for transfers between devices: 2.17 us -> 3.76 us  [swapped(): return lax.ppermute(value, axis, pairs)]
    ppermute x4 -> x5, starting transfers between devices: 28.1 us -> 28.8 us  [swapped(): return lax.ppermute(value, axis, pairs)]
  transfers between devices with their start and end apart: 4 -> 5, of which waited for: 2 -> 1; matrix products, arithmetic and copies ran while one was open for 1% -> 1% of each run, Pallas kernels for 8% -> 9%
where the time goes in v3:
time: 43.6 us; the launch traced here: 43.4 us
  starting transfers between devices  28.8 us (66%)
  Pallas kernels  9.91 us (23%)
  waiting for transfers between devices  3.76 us (9%)
  other arithmetic  0.53 us (1%)
    ppermute x5, starting transfers between devices, swapped(): return lax.ppermute(value, axis, pairs)  28.8 us
    pallas_call x1, Pallas kernels, middle_windows(): pl.pallas_call(middle_kernel, out_shape=(OUT, jax.ShapeDtypeStruct((288,...  4.11 us
    ppermute x5, waiting for transfers between devices, swapped(): return lax.ppermute(value, axis, pairs)  3.76 us
    pallas_call x1, Pallas kernels, expand(): pl.pallas_call(expand_kernel, out_shape=(half,) * 4 + (jax.ShapeDtypeStru...  3.53 us
    pallas_call x1, Pallas kernels, edge_windows(): pl.pallas_call(edge_kernel, out_shape=OUT, in_specs=[VMEM] * 10 + [HBM],...  2.28 us
  transfers between devices with their start and end apart: 5, of which 1 were waited for; matrix products, arithmetic and copies ran while one was open for 1% of the time, Pallas kernels for 9%

profile of v3, /device:TPU:31, one launch (start us, length us, event | category | flops | bytes accessed | tf_op | source)
XLA Modules:
  0.0 43.4 jit_solution(8392124418777350818)
XLA Ops:
  0.0 0.0 copy-start
  0.0 3.5 %expand.1 = (bf16[6,2,3,2,2,512]{5,4,3,2,1,0:T(2,128)(2,1)S(1)}, bf16[6,2,3,2,2,512]{5,4,3,2,1,0:T(2,128)(2,1)S(1)}, bf16[6,2,3,2,2,512]{5,4,3,2,1,0:T(2,128)(2,...) custom-call(bf16[6,6,2,1024]{3,2,1,0:T(2,128)(2,1)} %bitcast.38, bf16[1024,2048]{1,0:T(8,128)(2,1)} %weight.1, ...), custom_call_target="tpu_custom_call" | custom-call | flops 301989888 | bytes 5242880 | tf_op jit(solution)/shard_map/expand/pallas_call | solution.py:121
  3.5 2.6 %collective-permute-start = (bf16[12,6,2,512]{3,2,1,0:T(2,128)(2,1)S(1)}, bf16[12,6,2,512]{3,2,1,0:T(2,128)(2,1)S(1)}, u32[]{:S(2)}, u32[]{:S(2)}) collective-permute-start(bf16[12,6,2,512]{3,2,1,0:T(2,128)(2,1)S(1)} %bitcast.31), channel_id=1, source_target_pairs={{0,1},{1,0},{2,3},{3,2},{4,5},{5,4},{6,7},{7,6},{8,9},{9,8},{10,11... | collective-permute-start | bytes 442376 | tf_op jit(solution)/shard_map/ppermute | solution.py:349
  6.1 4.6 %collective-permute-start.1 = (bf16[12,6,2,512]{3,2,1,0:T(2,128)(2,1)S(1)}, bf16[12,6,2,512]{3,2,1,0:T(2,128)(2,1)S(1)}, u32[]{:S(2)}, u32[]{:S(2)}) collective-permute-start(bf16[12,6,2,512]{3,2,1,0:T(2,128)(2,1)S(1)} %bitcast.34), channel_id=1, source_target_pairs={{0,31},{1,2},{2,1},{3,4},{4,3},{5,6},{6,5},{7,8},{8,7},{9,10},{10,... | collective-permute-start | bytes 442376 | tf_op jit(solution)/shard_map/ppermute | solution.py:349
  10.7 0.1 dynamic-slice_bitcast_fusion.1
  10.9 0.0 collective-permute-done.beside0
  10.9 0.1 dynamic-slice_bitcast_fusion.2
  11.0 3.7 %collective-permute-done.1.beside1 = bf16[12,6,2,512]{3,2,1,0:T(2,128)(2,1)S(1)} collective-permute-done((bf16[12,6,2,512]{3,2,1,0:T(2,128)(2,1)S(1)}, bf16[12,6,2,512]{3,2,1,0:T(2,128)(2,1)S(1)}, u32[]{:S(2)}, u32[]{:S(2)}) %collective-permute-start.1) | collective-permute-done | bytes 147488 | tf_op jit(solution)/shard_map/ppermute | solution.py:349
  14.7 0.1 dynamic-slice_bitcast_fusion
  14.8 0.3 pad_maximum_fusion
  15.0 0.7 %collective-permute-start.3 = (bf16[4,3,6,2,512]{4,3,2,1,0:T(2,128)(2,1)S(1)}, bf16[4,3,6,2,512]{4,3,2,1,0:T(2,128)(2,1)S(1)}, u32[]{:S(2)}, u32[]{:S(2)}) collective-permute-start(bf16[4,3,6,2,512]{4,3,2,1,0:T(2,128)(2,1)S(1)} %pad_maximum_fusion), channel_id=1, source_target_pairs={{448,480},{480,448},{449,481},{481,449},{450,482},{482,450},{451,4... | collective-permute-start | bytes 442376 | tf_op jit(solution)/shard_map/ppermute | solution.py:349
  15.7 4.0 %collective-permute-start.2 = (bf16[4,3,6,2,512]{4,3,2,1,0:T(2,128)(2,1)S(1)}, bf16[4,3,6,2,512]{4,3,2,1,0:T(2,128)(2,1)S(1)}, u32[]{:S(2)}, u32[]{:S(2)}) collective-permute-start(bf16[4,3,6,2,512]{4,3,2,1,0:T(2,128)(2,1)S(1)} %pad_maximum_fusion), channel_id=1, source_target_pairs={{0,32},{32,0},{64,96},{96,64},{128,160},{160,128},{192,224},{224,1... | collective-permute-start | bytes 442376 | tf_op jit(solution)/shard_map/ppermute | solution.py:349
  19.7 0.3 pad_maximum_fusion.1
  20.0 17.0 %collective-permute-start.4 = (bf16[4,3,6,2,512]{4,3,2,1,0:T(2,128)(2,1)S(1)}, bf16[4,3,6,2,512]{4,3,2,1,0:T(2,128)(2,1)S(1)}, u32[]{:S(2)}, u32[]{:S(2)}) collective-permute-start(bf16[4,3,6,2,512]{4,3,2,1,0:T(2,128)(2,1)S(1)} %pad_maximum_fusion.1), channel_id=1, source_target_pairs={{0,0},{32,64},{64,32},{96,128},{128,96},{160,192},{192,160},{224,2... | collective-permute-start | bytes 442376 | tf_op jit(solution)/shard_map/ppermute | solution.py:349
  37.0 0.0 copy-done
  37.0 4.1 %middle.1 = (f32[12,12,2,512]{3,2,1,0:T(2,128)}, f32[288,512]{1,0:T(8,128)S(1)}, f32[288,512]{1,0:T(8,128)S(1)}, f32[160,512]{1,0:T(8,128)S(1)}, bf16[512,512]{1,0:T(8,128)(2,1)S(1)}) custom-call(bf16[12,6,2,512]{3,2,1,0:T(2,128)(2,1)S(1)} %bitcast.27, bf16[12,6,2,512]{3,2,1,0:T(2,128)(2,1)S(1)} %bitcast.29, bf16[12,6,2,512]{3,2,1,0:T(2,128)(2,1)S(1)} %bitcast.33, ...), custom_call_target="tpu_custom_call" | custom-call | flops 2147483648 | bytes 2097152 | tf_op jit(solution)/shard_map/middle/pallas_call | solution.py:296
  41.1 0.0 collective-permute-done.3.seam0
  41.1 0.0 collective-permute-done.2.over0
  41.1 0.0 collective-permute-done.4.over1
  41.1 2.3 %edges.1 = f32[12,12,2,512]{3,2,1,0:T(2,128)} custom-call(bf16[12,6,2,512]{3,2,1,0:T(2,128)(2,1)S(1)} %bitcast.28, bf16[12,6,2,512]{3,2,1,0:T(2,128)(2,1)S(1)} %bitcast.30, bf16[4,3,6,2,512]{4,3,2,1,0:T(2,128)(2,1)S(1)} %collective-permute-done.2.over0, bf16[4,3,6,2,512]{4,3,2,1,0:T(2,128)(2,1)S(1)} %collective-permute-done.3.seam0, ...), custom_call_target="tpu_custom_call", output_to_operand_aliasing={{}: (10, {})} | custom-call | flops 1073741824 | bytes 2097152 | tf_op jit(solution)/shard_map/edges/pallas_call | solution.py:320
Async XLA Ops:
  0.0 37.0 %copy-start = (f32[8]{0:T(128)S(1)}, f32[8]{0:T(128)}, u32[]{:S(2)}) copy-start(f32[8]{0:T(128)} %scale.1) | copy-start | bytes 100
  3.5 7.3 %collective-permute-start = (bf16[12,6,2,512]{3,2,1,0:T(2,128)(2,1)S(1)}, bf16[12,6,2,512]{3,2,1,0:T(2,128)(2,1)S(1)}, u32[]{:S(2)}, u32[]{:S(2)}) collective-permute-start(bf16[12,6,2,512]{3,2,1,0:T(2,128)(2,1)S(1)} %bitcast.31), channel_id=1, source_target_pairs={{0,1},{1,0},{2,3},{3,2},{4,5},{5,4},{6,7},{7,6},{8,9},{9,8},{10,11... | collective-permute-start | bytes 442376 | tf_op jit(solution)/shard_map/ppermute | solution.py:349
  6.1 8.6 %collective-permute-start.1 = (bf16[12,6,2,512]{3,2,1,0:T(2,128)(2,1)S(1)}, bf16[12,6,2,512]{3,2,1,0:T(2,128)(2,1)S(1)}, u32[]{:S(2)}, u32[]{:S(2)}) collective-permute-start(bf16[12,6,2,512]{3,2,1,0:T(2,128)(2,1)S(1)} %bitcast.34), channel_id=1, source_target_pairs={{0,31},{1,2},{2,1},{3,4},{4,3},{5,6},{6,5},{7,8},{8,7},{9,10},{10,... | collective-permute-start | bytes 442376 | tf_op jit(solution)/shard_map/ppermute | solution.py:349
  15.0 26.1 %collective-permute-start.3 = (bf16[4,3,6,2,512]{4,3,2,1,0:T(2,128)(2,1)S(1)}, bf16[4,3,6,2,512]{4,3,2,1,0:T(2,128)(2,1)S(1)}, u32[]{:S(2)}, u32[]{:S(2)}) collective-permute-start(bf16[4,3,6,2,512]{4,3,2,1,0:T(2,128)(2,1)S(1)} %pad_maximum_fusion), channel_id=1, source_target_pairs={{448,480},{480,448},{449,481},{481,449},{450,482},{482,450},{451,4... | collective-permute-start | bytes 442376 | tf_op jit(solution)/shard_map/ppermute | solution.py:349
  15.7 25.4 %collective-permute-start.2 = (bf16[4,3,6,2,512]{4,3,2,1,0:T(2,128)(2,1)S(1)}, bf16[4,3,6,2,512]{4,3,2,1,0:T(2,128)(2,1)S(1)}, u32[]{:S(2)}, u32[]{:S(2)}) collective-permute-start(bf16[4,3,6,2,512]{4,3,2,1,0:T(2,128)(2,1)S(1)} %pad_maximum_fusion), channel_id=1, source_target_pairs={{0,32},{32,0},{64,96},{96,64},{128,160},{160,128},{192,224},{224,1... | collective-permute-start | bytes 442376 | tf_op jit(solution)/shard_map/ppermute | solution.py:349
  20.0 21.1 %collective-permute-start.4 = (bf16[4,3,6,2,512]{4,3,2,1,0:T(2,128)(2,1)S(1)}, bf16[4,3,6,2,512]{4,3,2,1,0:T(2,128)(2,1)S(1)}, u32[]{:S(2)}, u32[]{:S(2)}) collective-permute-start(bf16[4,3,6,2,512]{4,3,2,1,0:T(2,128)(2,1)S(1)} %pad_maximum_fusion.1), channel_id=1, source_target_pairs={{0,0},{32,64},{64,32},{96,128},{128,96},{160,192},{192,160},{224,2... | collective-permute-start | bytes 442376 | tf_op jit(solution)/shard_map/ppermute | solution.py:349

commit v4 on v3

--- a/solution.py
+++ b/solution.py
@@ -201,52 +201,63 @@
     return bf16(result)
 
 
+def own_kernel(mine0, mine1, weight, scale, keys, values, queries):
+    lat = lax.axis_index("lat")
+    ones = head_ones()
+    centre = [pairs_of(mine[pl.ds(EDGE, ROWS - 2 * EDGE)]) for mine in (mine0, mine1)]
+    asking = list(centre)
+    for edge in (0, 1):
+        for mine in (mine0, mine1):
+            asking += [pairs_of(mine[pl.ds(edge_start(edge, lat), EDGE)]), centre[0][:2]]
+    asking = flat(jnp.concatenate(asking, axis=0))
+    middle = asking[:144]
+    for group in (0, 1):
+        lanes = slice(256 * group, 256 * group + 256)
+        queries[:, lanes] = scaled_queries(asking, weight, group, scale, ones)
+        keys[:, lanes] = unit(middle, weight, D + 256 * group, ones)
+        values[:, lanes] = projected(middle, weight, 2 * D + 256 * group).astype(jnp.float32)
+
+
 def middle_kernel(
-    own0, own1, mine0, mine1, beside0, beside1, weight, scale, projection, out, keys, values, queries, out_weight, every, made, blended, sent
+    own0, own1, mine0, mine1, beside0, beside1, weight, projection, own_keys, own_values, queries, *refs
 ):
+    made, keys, values, out_weight, blended, sent = refs
     lat, lon = lax.axis_index("lat"), lax.axis_index("lon")
     middle = pl.ds(EDGE, ROWS - 2 * EDGE)
     ones = head_ones()
-    fetched = pltpu.make_async_copy(projection, out_weight, sent.at[1])
+    fetched = pltpu.make_async_copy(projection, out_weight, sent)
     fetched.start()
-    asking = []
-    for half, mine, beside in ((0, mine0, beside0), (1, mine1, beside1)):
-        every[144 * half : 144 * half + 144] = flat(
-            jnp.concatenate([pairs_of(mine[middle]), pairs_of(beside[middle])], axis=0)
-        )
-        for edge in (0, 1):
-            rows = pl.ds(edge_start(edge, lat), EDGE)
-            at = 288 + 72 * (2 * edge + half)
-            every[at : at + 72] = flat(jnp.concatenate([pairs_of(mine[rows]), pairs_of(beside[rows])], axis=0))
-        asking.append(every[144 * half : 144 * half + 72])
-    asking += [every[288 + 72 * at : 288 + 72 * at + 40] for at in range(4)]
-    asking = bf16(jnp.concatenate([part.astype(jnp.float32) for part in asking], axis=0))
+    every = [pairs_of(beside[middle]) for beside in (beside0, beside1)]
+    for edge in (0, 1):
+        rows = pl.ds(edge_start(edge, lat), EDGE)
+        for mine, beside in ((mine0, beside0), (mine1, beside1)):
+            every += [pairs_of(mine[rows]), pairs_of(beside[rows])]
+    every = flat(jnp.concatenate(every, axis=0))
     for group in (0, 1):
         lanes = slice(256 * group, 256 * group + 256)
-        query = scaled_queries(asking, weight, group, scale, ones)
-        key = unit(every[...], weight, D + 256 * group, ones)
-        value = projected(every[...], weight, 2 * D + 256 * group)
+        key = unit(every, weight, D + 256 * group, ones)
+        value = projected(every, weight, 2 * D + 256 * group).astype(jnp.float32)
         for half in (0, 1):
-            window = slice(144 * half, 144 * half + 144)
-            blended[72 * half : 72 * half + 72, lanes] = attended(
-                query[72 * half : 72 * half + 72], bf16(key[window]), value[window]
+            part = slice(72 * half, 72 * half + 72)
+            blended[part, lanes] = attended(
+                queries[part, lanes],
+                bf16(jnp.concatenate([own_keys[part, lanes], key[part]], axis=0)),
+                bf16(jnp.concatenate([own_values[part, lanes], value[part]], axis=0)),
             )
-        keys[:, lanes] = key[288:]
-        values[:, lanes] = value[288:].astype(jnp.float32)
-        queries[:, lanes] = query[144:]
+        keys[:, lanes] = key[144:]
+        values[:, lanes] = value[144:]
     tokens = [flat(own[middle]).astype(jnp.float32) for own in (own0, own1)]
     fetched.wait()
     result = jnp.concatenate(tokens, axis=0) + dot(blended[...], out_weight[...])
     for half in (0, 1):
         made[:, pl.ds(half_start(half, lon), HALF)] = result[72 * half : 72 * half + 72].reshape(6, HALF, Z, D)
-    copy = pltpu.make_async_copy(made, out.at[middle], sent.at[0])
-    copy.start()
-    copy.wait()
 
 
 def edge_kernel(
     own0, own1, over0, seam0, over1, weight, out_weight, keys, values, queries, begun, out, made, blended, sent
 ):
+    earlier = pltpu.make_async_copy(begun, out.at[pl.ds(EDGE, ROWS - 2 * EDGE)], sent.at[2])
+    earlier.start()
     lat, lon = lax.axis_index("lat"), lax.axis_index("lon")
     last = lax.axis_size("lat") - 1
     ones = head_ones()
@@ -269,13 +280,13 @@
         for at in range(4):
             far = slice(72 * at, 72 * at + 72)
             blended[40 * at : 40 * at + 40, lanes] = attended(
-                queries[40 * at : 40 * at + 40, lanes],
+                queries[144 + 40 * at : 184 + 40 * at, lanes],
                 bf16(jnp.concatenate([keys[far, lanes], key[far]], axis=0)),
                 bf16(jnp.concatenate([values[far, lanes], value[far]], axis=0)),
                 live if at >= 2 else None,
             ).astype(jnp.float32)
     result = dot(bf16(blended[...]), out_weight[...])
-    copies = []
+    copies = [earlier]
     for edge in (0, 1):
         rows = pl.ds(edge_start(edge, lat), EDGE)
         for half, own in ((0, own0), (1, own1)):
@@ -283,51 +294,62 @@
             part = result[at : at + 40].reshape(20, Z, D)[:18].reshape(EDGE, HALF, Z, D)
             made[edge, :, pl.ds(half_start(half, lon), HALF)] = own[rows].astype(jnp.float32) + part
         copies.append(pltpu.make_async_copy(made.at[edge], out.at[rows], sent.at[edge]))
-    for copy in copies:
-        copy.start()
+        copies[-1].start()
     for copy in copies:
         copy.wait()
 
 
-OUT = jax.ShapeDtypeStruct((ROWS, COLS, Z, D), jnp.float32)
-
-
-def middle_windows(own, mine, beside, qkv_weight, logit_scale, out_weight):
+def own_parts(mine, qkv_weight, logit_scale):
+    shapes = ((144, D), (144, D), (304, D))
+    return pl.pallas_call(
+        own_kernel,
+        out_shape=tuple(jax.ShapeDtypeStruct(shape, jnp.float32) for shape in shapes),
+        in_specs=[VMEM] * 3 + [SMEM],
+        out_specs=(VMEM,) * 3,
+        compiler_params=pltpu.CompilerParams(vmem_limit_bytes=32 * MIB),
+        cost_estimate=pl.CostEstimate(flops=1 << 30, bytes_accessed=2 * MIB, transcendentals=0),
+        name="own",
+    )(*mine, qkv_weight, logit_scale)
+
+
+def middle_windows(own, mine, beside, qkv_weight, out_weight, keys, values, queries):
     return pl.pallas_call(
         middle_kernel,
         out_shape=(
-            OUT,
+            jax.ShapeDtypeStruct((6, COLS, Z, D), jnp.float32),
             jax.ShapeDtypeStruct((288, D), jnp.float32),
             jax.ShapeDtypeStruct((288, D), jnp.float32),
-            jax.ShapeDtypeStruct((160, D), jnp.float32),
             jax.ShapeDtypeStruct((D, D), jnp.bfloat16),
         ),
-        in_specs=[VMEM] * 7 + [SMEM, HBM],
-        out_specs=(HBM, VMEM, VMEM, VMEM, VMEM),
-        scratch_shapes=[
-            pltpu.VMEM((576, D), jnp.bfloat16),
-            pltpu.VMEM((6, COLS, Z, D), jnp.float32),
-            pltpu.VMEM((144, D), jnp.bfloat16),
-            pltpu.SemaphoreType.DMA((2,)),
-        ],
+        in_specs=[VMEM] * 7 + [HBM] + [VMEM] * 3,
+        out_specs=(VMEM,) * 4,
+        scratch_shapes=[pltpu.VMEM((144, D), jnp.bfloat16), pltpu.SemaphoreType.DMA(())],
         compiler_params=pltpu.CompilerParams(vmem_limit_bytes=32 * MIB),
         cost_estimate=pl.CostEstimate(flops=2 << 30, bytes_accessed=2 * MIB, transcendentals=350000),
         name="middle",
-    )(*own, *mine, *beside, qkv_weight, logit_scale, pltpu.with_memory_space_constraint(out_weight, pltpu.HBM))
+    )(
+        *own,
+        *mine,
+        *beside,
+        qkv_weight,
+        pltpu.with_memory_space_constraint(out_weight, pltpu.HBM),
+        keys,
+        values,
+        queries,
+    )
 
 
 def edge_windows(own, over, qkv_weight, begun, keys, values, queries, out_weight):
     return pl.pallas_call(
         edge_kernel,
-        out_shape=OUT,
-        in_specs=[VMEM] * 10 + [HBM],
+        out_shape=jax.ShapeDtypeStruct((ROWS, COLS, Z, D), jnp.float32),
+        in_specs=[VMEM] * 11,
         out_specs=HBM,
         scratch_shapes=[
             pltpu.VMEM((2, EDGE, COLS, Z, D), jnp.float32),
             pltpu.VMEM((160, D), jnp.float32),
-            pltpu.SemaphoreType.DMA((2,)),
+            pltpu.SemaphoreType.DMA((3,)),
         ],
-        input_output_aliases={10: 0},
         compiler_params=pltpu.CompilerParams(vmem_limit_bytes=32 * MIB),
         cost_estimate=pl.CostEstimate(flops=1 << 30, bytes_accessed=2 * MIB, transcendentals=350000),
         name="edges",
@@ -364,6 +386,7 @@
     own, mine, qkv_weight = expand(
         coarse, skip_tokens, land_sea, surf_table, expand_weight, expand_gain, attn_gain, qkv_weight
     )
+    own_keys, own_values, queries = own_parts(mine, qkv_weight, logit_scale)
     beside = []
     for turn in (0, 1):
         beside.append(swapped(mine[turn], "lon", turn, True))
@@ -384,8 +407,10 @@
     over1 = swapped(rows[1], "lat", 1, False)
     seam0 = swapped(rows[0], "lat", 0, False, at_seam)
     over = (over0, seam0, over1)
-    begun, *held = middle_windows(own, mine, beside, qkv_weight, logit_scale, out_weight)
-    mixed = edge_windows(own, over, qkv_weight, begun, *held)
+    begun, keys, values, out_weight = middle_windows(
+        own, mine, beside, qkv_weight, out_weight, own_keys, own_values, queries
+    )
+    mixed = edge_windows(own, over, qkv_weight, begun, keys, values, queries, out_weight)
     return jnp.transpose(mixed, (2, 0, 1, 3))
 
 

time: 43.6 us -> 42.4 us (0.972)
  the two profiles are of different devices: /device:TPU:31 before, /device:TPU:47 now
where the time goes in v4:
time: 42.4 us; the launch traced here: 42.2 us
  starting transfers between devices  26.7 us (63%)
  Pallas kernels  9.27 us (22%)
  waiting for transfers between devices  5.27 us (12%)
  other arithmetic  0.53 us (1%)
    ppermute x5, starting transfers between devices, swapped(): return lax.ppermute(value, axis, pairs)  26.7 us
    ppermute x5, waiting for transfers between devices, swapped(): return lax.ppermute(value, axis, pairs)  5.27 us
    pallas_call x1, Pallas kernels, expand(): pl.pallas_call(expand_kernel, out_shape=(half,) * 4 + (jax.ShapeDtypeStru...  3.53 us
    pallas_call x1, Pallas kernels, edge_windows(): pl.pallas_call(edge_kernel, out_shape=jax.ShapeDtypeStruct((ROWS, COLS, Z...  2.23 us
    pallas_call x1, Pallas kernels, middle_windows(): pl.pallas_call(middle_kernel, out_shape=(jax.ShapeDtypeStruct((6, COLS, Z...  1.88 us
    pallas_call x1, Pallas kernels, own_parts(): pl.pallas_call(own_kernel, out_shape=tuple((jax.ShapeDtypeStruct(shape, j...  1.63 us
  transfers between devices with their start and end apart: 5, of which 2 were waited for; matrix products, arithmetic and copies ran while one was open for 1% of the time, Pallas kernels for 8%

profile of v4, /device:TPU:47, one launch (start us, length us, event | category | flops | bytes accessed | tf_op | source)
XLA Modules:
  0.0 42.2 jit_solution(15147809617854438464)
XLA Ops:
  0.0 0.0 copy-start
  0.0 3.5 %expand.1 = (bf16[6,2,3,2,2,512]{5,4,3,2,1,0:T(2,128)(2,1)S(1)}, bf16[6,2,3,2,2,512]{5,4,3,2,1,0:T(2,128)(2,1)S(1)}, bf16[6,2,3,2,2,512]{5,4,3,2,1,0:T(2,128)(2,...) custom-call(bf16[6,6,2,1024]{3,2,1,0:T(2,128)(2,1)} %bitcast.40, bf16[1024,2048]{1,0:T(8,128)(2,1)} %weight.1, ...), custom_call_target="tpu_custom_call" | custom-call | flops 301989888 | bytes 5242880 | tf_op jit(solution)/shard_map/expand/pallas_call | solution.py:121
  3.5 2.6 %collective-permute-start = (bf16[12,6,2,512]{3,2,1,0:T(2,128)(2,1)S(1)}, bf16[12,6,2,512]{3,2,1,0:T(2,128)(2,1)S(1)}, u32[]{:S(2)}, u32[]{:S(2)}) collective-permute-start(bf16[12,6,2,512]{3,2,1,0:T(2,128)(2,1)S(1)} %bitcast.31), channel_id=1, source_target_pairs={{0,1},{1,0},{2,3},{3,2},{4,5},{5,4},{6,7},{7,6},{8,9},{9,8},{10,11... | collective-permute-start | bytes 442376 | tf_op jit(solution)/shard_map/ppermute | solution.py:371
  6.1 2.5 %collective-permute-start.1 = (bf16[12,6,2,512]{3,2,1,0:T(2,128)(2,1)S(1)}, bf16[12,6,2,512]{3,2,1,0:T(2,128)(2,1)S(1)}, u32[]{:S(2)}, u32[]{:S(2)}) collective-permute-start(bf16[12,6,2,512]{3,2,1,0:T(2,128)(2,1)S(1)} %bitcast.35), channel_id=1, source_target_pairs={{0,31},{1,2},{2,1},{3,4},{4,3},{5,6},{6,5},{7,8},{8,7},{9,10},{10,... | collective-permute-start | bytes 442376 | tf_op jit(solution)/shard_map/ppermute | solution.py:371
  8.6 0.1 dynamic-slice_bitcast_fusion.1
  8.8 0.0 copy-done
  8.8 1.6 %own.1 = (f32[144,512]{1,0:T(8,128)S(1)}, f32[144,512]{1,0:T(8,128)S(1)}, f32[304,512]{1,0:T(8,128)S(1)}) custom-call(bf16[12,6,2,512]{3,2,1,0:T(2,128)(2,1)S(1)} %bitcast.33, bf16[12,6,2,512]{3,2,1,0:T(2,128)(2,1)S(1)} %bitcast.37, bf16[512,1536]{1,0:T(8,128)(2,1)S(1)} %get-tuple-element.21.weight, f32[8]{0:T(128)S(1)} %copy-done), custom_call_target="tpu_custom_call" | custom-call | flops 1073741824 | bytes 2097152 | tf_op jit(solution)/shard_map/own/pallas_call | solution.py:304
  10.4 0.0 collective-permute-done.beside0
  10.4 0.1 dynamic-slice_bitcast_fusion.2
  10.5 3.0 %collective-permute-done.1.beside1 = bf16[12,6,2,512]{3,2,1,0:T(2,128)(2,1)S(1)} collective-permute-done((bf16[12,6,2,512]{3,2,1,0:T(2,128)(2,1)S(1)}, bf16[12,6,2,512]{3,2,1,0:T(2,128)(2,1)S(1)}, u32[]{:S(2)}, u32[]{:S(2)}) %collective-permute-start.1) | collective-permute-done | bytes 147488 | tf_op jit(solution)/shard_map/ppermute | solution.py:371
  13.5 0.1 dynamic-slice_bitcast_fusion
  13.6 0.3 pad_maximum_fusion
  13.8 4.0 %collective-permute-start.2 = (bf16[4,3,6,2,512]{4,3,2,1,0:T(2,128)(2,1)S(1)}, bf16[4,3,6,2,512]{4,3,2,1,0:T(2,128)(2,1)S(1)}, u32[]{:S(2)}, u32[]{:S(2)}) collective-permute-start(bf16[4,3,6,2,512]{4,3,2,1,0:T(2,128)(2,1)S(1)} %pad_maximum_fusion), channel_id=1, source_target_pairs={{0,32},{32,0},{64,96},{96,64},{128,160},{160,128},{192,224},{224,1... | collective-permute-start | bytes 442376 | tf_op jit(solution)/shard_map/ppermute | solution.py:371
  17.8 0.7 %collective-permute-start.3 = (bf16[4,3,6,2,512]{4,3,2,1,0:T(2,128)(2,1)S(1)}, bf16[4,3,6,2,512]{4,3,2,1,0:T(2,128)(2,1)S(1)}, u32[]{:S(2)}, u32[]{:S(2)}) collective-permute-start(bf16[4,3,6,2,512]{4,3,2,1,0:T(2,128)(2,1)S(1)} %pad_maximum_fusion), channel_id=1, source_target_pairs={{448,480},{480,448},{449,481},{481,449},{450,482},{482,450},{451,4... | collective-permute-start | bytes 442376 | tf_op jit(solution)/shard_map/ppermute | solution.py:371
  18.5 0.3 pad_maximum_fusion.1
  18.8 17.0 %collective-permute-start.4 = (bf16[4,3,6,2,512]{4,3,2,1,0:T(2,128)(2,1)S(1)}, bf16[4,3,6,2,512]{4,3,2,1,0:T(2,128)(2,1)S(1)}, u32[]{:S(2)}, u32[]{:S(2)}) collective-permute-start(bf16[4,3,6,2,512]{4,3,2,1,0:T(2,128)(2,1)S(1)} %pad_maximum_fusion.1), channel_id=1, source_target_pairs={{0,0},{32,64},{64,32},{96,128},{128,96},{160,192},{192,160},{224,2... | collective-permute-start | bytes 442376 | tf_op jit(solution)/shard_map/ppermute | solution.py:371
  35.8 1.9 %middle.1 = (f32[6,12,2,512]{3,2,1,0:T(2,128)S(1)}, f32[288,512]{1,0:T(8,128)S(1)}, f32[288,512]{1,0:T(8,128)S(1)}, bf16[512,512]{1,0:T(8,128)(2,1)S(1)}) custom-call(bf16[12,6,2,512]{3,2,1,0:T(2,128)(2,1)S(1)} %bitcast.27, bf16[12,6,2,512]{3,2,1,0:T(2,128)(2,1)S(1)} %bitcast.29, bf16[12,6,2,512]{3,2,1,0:T(2,128)(2,1)S(1)} %bitcast.34, ...), custom_call_target="tpu_custom_call" | custom-call | flops 2147483648 | bytes 2097152 | tf_op jit(solution)/shard_map/middle/pallas_call | solution.py:316
  37.7 2.3 %collective-permute-done.4.over1 = bf16[4,3,6,2,512]{4,3,2,1,0:T(2,128)(2,1)S(1)} collective-permute-done((bf16[4,3,6,2,512]{4,3,2,1,0:T(2,128)(2,1)S(1)}, bf16[4,3,6,2,512]{4,3,2,1,0:T(2,128)(2,1)S(1)}, u32[]{:S(2)}, u32[]{:S(2)}) %collective-permute-start.4) | collective-permute-done | bytes 147488 | tf_op jit(solution)/shard_map/ppermute | solution.py:371
  39.9 0.0 collective-permute-done.2.over0
  39.9 0.0 collective-permute-done.3.seam0
  39.9 2.2 %edges.1 = f32[12,12,2,512]{3,2,1,0:T(2,128)} custom-call(bf16[12,6,2,512]{3,2,1,0:T(2,128)(2,1)S(1)} %bitcast.28, bf16[12,6,2,512]{3,2,1,0:T(2,128)(2,1)S(1)} %bitcast.30, bf16[4,3,6,2,512]{4,3,2,1,0:T(2,128)(2,1)S(1)} %collective-permute-done.2.over0, bf16[4,3,6,2,512]{4,3,2,1,0:T(2,128)(2,1)S(1)} %collective-permute-done.3.seam0, ...), custom_call_target="tpu_custom_call" | custom-call | flops 1073741824 | bytes 2097152 | tf_op jit(solution)/shard_map/edges/pallas_call | solution.py:343
Async XLA Ops:
  0.0 8.8 %copy-start = (f32[8]{0:T(128)S(1)}, f32[8]{0:T(128)}, u32[]{:S(2)}) copy-start(f32[8]{0:T(128)} %scale.1) | copy-start | bytes 100
  3.5 6.9 %collective-permute-start = (bf16[12,6,2,512]{3,2,1,0:T(2,128)(2,1)S(1)}, bf16[12,6,2,512]{3,2,1,0:T(2,128)(2,1)S(1)}, u32[]{:S(2)}, u32[]{:S(2)}) collective-permute-start(bf16[12,6,2,512]{3,2,1,0:T(2,128)(2,1)S(1)} %bitcast.31), channel_id=1, source_target_pairs={{0,1},{1,0},{2,3},{3,2},{4,5},{5,4},{6,7},{7,6},{8,9},{9,8},{10,11... | collective-permute-start | bytes 442376 | tf_op jit(solution)/shard_map/ppermute | solution.py:371
  6.1 7.4 %collective-permute-start.1 = (bf16[12,6,2,512]{3,2,1,0:T(2,128)(2,1)S(1)}, bf16[12,6,2,512]{3,2,1,0:T(2,128)(2,1)S(1)}, u32[]{:S(2)}, u32[]{:S(2)}) collective-permute-start(bf16[12,6,2,512]{3,2,1,0:T(2,128)(2,1)S(1)} %bitcast.35), channel_id=1, source_target_pairs={{0,31},{1,2},{2,1},{3,4},{4,3},{5,6},{6,5},{7,8},{8,7},{9,10},{10,... | collective-permute-start | bytes 442376 | tf_op jit(solution)/shard_map/ppermute | solution.py:371
  13.8 26.1 %collective-permute-start.2 = (bf16[4,3,6,2,512]{4,3,2,1,0:T(2,128)(2,1)S(1)}, bf16[4,3,6,2,512]{4,3,2,1,0:T(2,128)(2,1)S(1)}, u32[]{:S(2)}, u32[]{:S(2)}) collective-permute-start(bf16[4,3,6,2,512]{4,3,2,1,0:T(2,128)(2,1)S(1)} %pad_maximum_fusion), channel_id=1, source_target_pairs={{0,32},{32,0},{64,96},{96,64},{128,160},{160,128},{192,224},{224,1... | collective-permute-start | bytes 442376 | tf_op jit(solution)/shard_map/ppermute | solution.py:371
  17.8 22.1 %collective-permute-start.3 = (bf16[4,3,6,2,512]{4,3,2,1,0:T(2,128)(2,1)S(1)}, bf16[4,3,6,2,512]{4,3,2,1,0:T(2,128)(2,1)S(1)}, u32[]{:S(2)}, u32[]{:S(2)}) collective-permute-start(bf16[4,3,6,2,512]{4,3,2,1,0:T(2,128)(2,1)S(1)} %pad_maximum_fusion), channel_id=1, source_target_pairs={{448,480},{480,448},{449,481},{481,449},{450,482},{482,450},{451,4... | collective-permute-start | bytes 442376 | tf_op jit(solution)/shard_map/ppermute | solution.py:371
  18.8 21.1 %collective-permute-start.4 = (bf16[4,3,6,2,512]{4,3,2,1,0:T(2,128)(2,1)S(1)}, bf16[4,3,6,2,512]{4,3,2,1,0:T(2,128)(2,1)S(1)}, u32[]{:S(2)}, u32[]{:S(2)}) collective-permute-start(bf16[4,3,6,2,512]{4,3,2,1,0:T(2,128)(2,1)S(1)} %pad_maximum_fusion.1), channel_id=1, source_target_pairs={{0,0},{32,64},{64,32},{96,128},{128,96},{160,192},{192,160},{224,2... | collective-permute-start | bytes 442376 | tf_op jit(solution)/shard_map/ppermute | solution.py:371

commit v5 on v4

--- a/solution.py
+++ b/solution.py
@@ -201,51 +201,37 @@
     return bf16(result)
 
 
-def own_kernel(mine0, mine1, weight, scale, keys, values, queries):
-    lat = lax.axis_index("lat")
-    ones = head_ones()
-    centre = [pairs_of(mine[pl.ds(EDGE, ROWS - 2 * EDGE)]) for mine in (mine0, mine1)]
-    asking = list(centre)
-    for edge in (0, 1):
-        for mine in (mine0, mine1):
-            asking += [pairs_of(mine[pl.ds(edge_start(edge, lat), EDGE)]), centre[0][:2]]
-    asking = flat(jnp.concatenate(asking, axis=0))
-    middle = asking[:144]
-    for group in (0, 1):
-        lanes = slice(256 * group, 256 * group + 256)
-        queries[:, lanes] = scaled_queries(asking, weight, group, scale, ones)
-        keys[:, lanes] = unit(middle, weight, D + 256 * group, ones)
-        values[:, lanes] = projected(middle, weight, 2 * D + 256 * group).astype(jnp.float32)
-
-
-def middle_kernel(
-    own0, own1, mine0, mine1, beside0, beside1, weight, projection, own_keys, own_values, queries, *refs
-):
-    made, keys, values, out_weight, blended, sent = refs
+def middle_kernel(own0, own1, mine0, mine1, beside0, beside1, weight, scale, projection, *refs):
+    made, keys, values, queries, out_weight, blended, sent = refs
     lat, lon = lax.axis_index("lat"), lax.axis_index("lon")
     middle = pl.ds(EDGE, ROWS - 2 * EDGE)
     ones = head_ones()
     fetched = pltpu.make_async_copy(projection, out_weight, sent)
     fetched.start()
-    every = [pairs_of(beside[middle]) for beside in (beside0, beside1)]
+    every, asking = [], []
+    for mine, beside in ((mine0, beside0), (mine1, beside1)):
+        asking.append(pairs_of(mine[middle]))
+        every += [asking[-1], pairs_of(beside[middle])]
     for edge in (0, 1):
         rows = pl.ds(edge_start(edge, lat), EDGE)
         for mine, beside in ((mine0, beside0), (mine1, beside1)):
+            asking += [pairs_of(mine[rows]), asking[0][:2]]
             every += [pairs_of(mine[rows]), pairs_of(beside[rows])]
     every = flat(jnp.concatenate(every, axis=0))
+    asking = flat(jnp.concatenate(asking, axis=0))
     for group in (0, 1):
         lanes = slice(256 * group, 256 * group + 256)
+        query = scaled_queries(asking, weight, group, scale, ones)
         key = unit(every, weight, D + 256 * group, ones)
-        value = projected(every, weight, 2 * D + 256 * group).astype(jnp.float32)
+        value = projected(every, weight, 2 * D + 256 * group)
         for half in (0, 1):
-            part = slice(72 * half, 72 * half + 72)
-            blended[part, lanes] = attended(
-                queries[part, lanes],
-                bf16(jnp.concatenate([own_keys[part, lanes], key[part]], axis=0)),
-                bf16(jnp.concatenate([own_values[part, lanes], value[part]], axis=0)),
+            window = slice(144 * half, 144 * half + 144)
+            blended[72 * half : 72 * half + 72, lanes] = attended(
+                query[72 * half : 72 * half + 72], bf16(key[window]), value[window]
             )
-        keys[:, lanes] = key[144:]
-        values[:, lanes] = value[144:]
+        keys[:, lanes] = key[288:]
+        values[:, lanes] = value[288:].astype(jnp.float32)
+        queries[:, lanes] = query[144:]
     tokens = [flat(own[middle]).astype(jnp.float32) for own in (own0, own1)]
     fetched.wait()
     result = jnp.concatenate(tokens, axis=0) + dot(blended[...], out_weight[...])
@@ -280,7 +266,7 @@
         for at in range(4):
             far = slice(72 * at, 72 * at + 72)
             blended[40 * at : 40 * at + 40, lanes] = attended(
-                queries[144 + 40 * at : 184 + 40 * at, lanes],
+                queries[40 * at : 40 * at + 40, lanes],
                 bf16(jnp.concatenate([keys[far, lanes], key[far]], axis=0)),
                 bf16(jnp.concatenate([values[far, lanes], value[far]], axis=0)),
                 live if at >= 2 else None,
@@ -299,30 +285,38 @@
         copy.wait()
 
 
-def own_parts(mine, qkv_weight, logit_scale):
-    shapes = ((144, D), (144, D), (304, D))
+def pack_kernel(mine0, mine1, beside0, beside1, rows0, rows1):
+    lat = lax.axis_index("lat")
+    for turn, rows in ((0, rows0), (1, rows1)):
+        edge = pl.ds(edge_start(turn, lat), EDGE)
+        for at, part in enumerate((mine0, beside0, mine1, beside1)):
+            rows[at] = part[edge]
+
+
+def edge_rows(mine, beside):
     return pl.pallas_call(
-        own_kernel,
-        out_shape=tuple(jax.ShapeDtypeStruct(shape, jnp.float32) for shape in shapes),
-        in_specs=[VMEM] * 3 + [SMEM],
-        out_specs=(VMEM,) * 3,
-        compiler_params=pltpu.CompilerParams(vmem_limit_bytes=32 * MIB),
-        cost_estimate=pl.CostEstimate(flops=1 << 30, bytes_accessed=2 * MIB, transcendentals=0),
-        name="own",
-    )(*mine, qkv_weight, logit_scale)
-
-
-def middle_windows(own, mine, beside, qkv_weight, out_weight, keys, values, queries):
+        pack_kernel,
+        out_shape=(jax.ShapeDtypeStruct((4, EDGE, HALF, Z, D), jnp.bfloat16),) * 2,
+        in_specs=[VMEM] * 4,
+        out_specs=(VMEM,) * 2,
+        compiler_params=pltpu.CompilerParams(vmem_limit_bytes=8 * MIB),
+        cost_estimate=pl.CostEstimate(flops=1000, bytes_accessed=MIB // 4, transcendentals=0),
+        name="pack",
+    )(*mine, *beside)
+
+
+def middle_windows(own, mine, beside, qkv_weight, logit_scale, out_weight):
     return pl.pallas_call(
         middle_kernel,
         out_shape=(
             jax.ShapeDtypeStruct((6, COLS, Z, D), jnp.float32),
             jax.ShapeDtypeStruct((288, D), jnp.float32),
             jax.ShapeDtypeStruct((288, D), jnp.float32),
+            jax.ShapeDtypeStruct((160, D), jnp.float32),
             jax.ShapeDtypeStruct((D, D), jnp.bfloat16),
         ),
-        in_specs=[VMEM] * 7 + [HBM] + [VMEM] * 3,
-        out_specs=(VMEM,) * 4,
+        in_specs=[VMEM] * 7 + [SMEM, HBM],
+        out_specs=(VMEM,) * 5,
         scratch_shapes=[pltpu.VMEM((144, D), jnp.bfloat16), pltpu.SemaphoreType.DMA(())],
         compiler_params=pltpu.CompilerParams(vmem_limit_bytes=32 * MIB),
         cost_estimate=pl.CostEstimate(flops=2 << 30, bytes_accessed=2 * MIB, transcendentals=350000),
@@ -332,10 +326,8 @@
         *mine,
         *beside,
         qkv_weight,
+        logit_scale,
         pltpu.with_memory_space_constraint(out_weight, pltpu.HBM),
-        keys,
-        values,
-        queries,
     )
 
 
@@ -386,30 +378,17 @@
     own, mine, qkv_weight = expand(
         coarse, skip_tokens, land_sea, surf_table, expand_weight, expand_gain, attn_gain, qkv_weight
     )
-    own_keys, own_values, queries = own_parts(mine, qkv_weight, logit_scale)
     beside = []
     for turn in (0, 1):
         beside.append(swapped(mine[turn], "lon", turn, True))
-    lat = lax.axis_index("lat")
-
-    def rows_for(turn):
-        return jnp.stack(
-            [
-                lax.dynamic_slice_in_dim(part, edge_start(turn, lat), EDGE, 0)
-                for part in (mine[0], beside[0], mine[1], beside[1])
-            ]
-        )
-
     seam = seam_of("lat")
     at_seam = [seam - 1, seam]
-    rows = [rows_for(turn) for turn in (0, 1)]
+    rows = edge_rows(mine, beside)
     over0 = swapped(rows[0], "lat", 0, False, [at for at in range(lax.axis_size("lat")) if at not in at_seam])
     over1 = swapped(rows[1], "lat", 1, False)
     seam0 = swapped(rows[0], "lat", 0, False, at_seam)
     over = (over0, seam0, over1)
-    begun, keys, values, out_weight = middle_windows(
-        own, mine, beside, qkv_weight, out_weight, own_keys, own_values, queries
-    )
+    begun, keys, values, queries, out_weight = middle_windows(own, mine, beside, qkv_weight, logit_scale, out_weight)
     mixed = edge_windows(own, over, qkv_weight, begun, keys, values, queries, out_weight)
     return jnp.transpose(mixed, (2, 0, 1, 3))
 

time: 42.4 us -> 42.3 us (level)
  the two profiles are of different devices: /device:TPU:47 before, /device:TPU:31 now
where the time goes in v5:
time: 42.3 us; the launch traced here: 42.1 us
  starting transfers between devices  28.8 us (68%)
  Pallas kernels  9.19 us (22%)
  waiting for transfers between devices  3.99 us (9%)
    ppermute x5, starting transfers between devices, swapped(): return lax.ppermute(value, axis, pairs)  28.8 us
    ppermute x5, waiting for transfers between devices, swapped(): return lax.ppermute(value, axis, pairs)  3.99 us
    pallas_call x1, Pallas kernels, expand(): pl.pallas_call(expand_kernel, out_shape=(half,) * 4 + (jax.ShapeDtypeStru...  3.53 us
    pallas_call x1, Pallas kernels, middle_windows(): pl.pallas_call(middle_kernel, out_shape=(jax.ShapeDtypeStruct((6, COLS, Z...  3.4 us
    pallas_call x1, Pallas kernels, edge_windows(): pl.pallas_call(edge_kernel, out_shape=jax.ShapeDtypeStruct((ROWS, COLS, Z...  2.24 us
  transfers between devices with their start and end apart: 5, of which 1 were waited for; matrix products, arithmetic and copies ran while one was open for 0% of the time, Pallas kernels for 8%

profile of v5, /device:TPU:31, one launch (start us, length us, event | category | flops | bytes accessed | tf_op | source)
XLA Modules:
  0.0 42.1 jit_solution(9129139211687410490)
XLA Ops:
  0.0 0.0 copy-start
  0.0 3.5 %expand.1 = (bf16[6,2,3,2,2,512]{5,4,3,2,1,0:T(2,128)(2,1)S(1)}, bf16[6,2,3,2,2,512]{5,4,3,2,1,0:T(2,128)(2,1)S(1)}, bf16[6,2,3,2,2,512]{5,4,3,2,1,0:T(2,128)(2,...) custom-call(bf16[6,6,2,1024]{3,2,1,0:T(2,128)(2,1)} %bitcast.22, bf16[1024,2048]{1,0:T(8,128)(2,1)} %weight.1, ...), custom_call_target="tpu_custom_call" | custom-call | flops 301989888 | bytes 5242880 | tf_op jit(solution)/shard_map/expand/pallas_call | solution.py:121
  3.5 2.6 %collective-permute-start = (bf16[12,6,2,512]{3,2,1,0:T(2,128)(2,1)S(1)}, bf16[12,6,2,512]{3,2,1,0:T(2,128)(2,1)S(1)}, u32[]{:S(2)}, u32[]{:S(2)}) collective-permute-start(bf16[12,6,2,512]{3,2,1,0:T(2,128)(2,1)S(1)} %bitcast.15), channel_id=1, source_target_pairs={{0,1},{1,0},{2,3},{3,2},{4,5},{5,4},{6,7},{7,6},{8,9},{9,8},{10,11... | collective-permute-start | bytes 442376 | tf_op jit(solution)/shard_map/ppermute | solution.py:363
  6.1 4.6 %collective-permute-start.1 = (bf16[12,6,2,512]{3,2,1,0:T(2,128)(2,1)S(1)}, bf16[12,6,2,512]{3,2,1,0:T(2,128)(2,1)S(1)}, u32[]{:S(2)}, u32[]{:S(2)}) collective-permute-start(bf16[12,6,2,512]{3,2,1,0:T(2,128)(2,1)S(1)} %bitcast.18), channel_id=1, source_target_pairs={{0,31},{1,2},{2,1},{3,4},{4,3},{5,6},{6,5},{7,8},{8,7},{9,10},{10,... | collective-permute-start | bytes 442376 | tf_op jit(solution)/shard_map/ppermute | solution.py:363
  10.7 0.0 collective-permute-done.beside0
  10.7 4.0 %collective-permute-done.1.beside1 = bf16[12,6,2,512]{3,2,1,0:T(2,128)(2,1)S(1)} collective-permute-done((bf16[12,6,2,512]{3,2,1,0:T(2,128)(2,1)S(1)}, bf16[12,6,2,512]{3,2,1,0:T(2,128)(2,1)S(1)}, u32[]{:S(2)}, u32[]{:S(2)}) %collective-permute-start.1) | collective-permute-done | bytes 147488 | tf_op jit(solution)/shard_map/ppermute | solution.py:363
  14.7 4.0 %collective-permute-start.2 = (bf16[4,3,6,2,512]{4,3,2,1,0:T(2,128)(2,1)S(1)}, bf16[4,3,6,2,512]{4,3,2,1,0:T(2,128)(2,1)S(1)}, u32[]{:S(2)}, u32[]{:S(2)}) collective-permute-start(bf16[4,3,6,2,512]{4,3,2,1,0:T(2,128)(2,1)S(1)} %get-tuple-element.21), channel_id=1, source_target_pairs={{0,32},{32,0},{64,96},{96,64},{128,160},{160,128},{192,224},{224,1... | collective-permute-start | bytes 442376 | tf_op jit(solution)/shard_map/ppermute | solution.py:363
  18.7 0.7 %collective-permute-start.3 = (bf16[4,3,6,2,512]{4,3,2,1,0:T(2,128)(2,1)S(1)}, bf16[4,3,6,2,512]{4,3,2,1,0:T(2,128)(2,1)S(1)}, u32[]{:S(2)}, u32[]{:S(2)}) collective-permute-start(bf16[4,3,6,2,512]{4,3,2,1,0:T(2,128)(2,1)S(1)} %get-tuple-element.21), channel_id=1, source_target_pairs={{448,480},{480,448},{449,481},{481,449},{450,482},{482,450},{451,4... | collective-permute-start | bytes 442376 | tf_op jit(solution)/shard_map/ppermute | solution.py:363
  19.4 17.0 %collective-permute-start.4 = (bf16[4,3,6,2,512]{4,3,2,1,0:T(2,128)(2,1)S(1)}, bf16[4,3,6,2,512]{4,3,2,1,0:T(2,128)(2,1)S(1)}, u32[]{:S(2)}, u32[]{:S(2)}) collective-permute-start(bf16[4,3,6,2,512]{4,3,2,1,0:T(2,128)(2,1)S(1)} %get-tuple-element.22), channel_id=1, source_target_pairs={{0,0},{32,64},{64,32},{96,128},{128,96},{160,192},{192,160},{224,2... | collective-permute-start | bytes 442376 | tf_op jit(solution)/shard_map/ppermute | solution.py:363
  36.4 0.0 copy-done
  36.4 3.4 %middle.1 = (f32[6,12,2,512]{3,2,1,0:T(2,128)S(1)}, f32[288,512]{1,0:T(8,128)S(1)}, f32[288,512]{1,0:T(8,128)S(1)}, f32[160,512]{1,0:T(8,128)S(1)}, bf16[512,512]{1,0:T(8,128)(2,1)S(1)}) custom-call(bf16[12,6,2,512]{3,2,1,0:T(2,128)(2,1)S(1)} %bitcast.11, bf16[12,6,2,512]{3,2,1,0:T(2,128)(2,1)S(1)} %bitcast.13, bf16[12,6,2,512]{3,2,1,0:T(2,128)(2,1)S(1)} %bitcast.17, ...), custom_call_target="tpu_custom_call" | custom-call | flops 2147483648 | bytes 2097152 | tf_op jit(solution)/shard_map/middle/pallas_call | solution.py:309
  39.8 0.0 collective-permute-done.2.over0
  39.8 0.0 collective-permute-done.3.seam0
  39.8 0.0 collective-permute-done.4.over1
  39.8 2.2 %edges.1 = f32[12,12,2,512]{3,2,1,0:T(2,128)} custom-call(bf16[12,6,2,512]{3,2,1,0:T(2,128)(2,1)S(1)} %bitcast.12, bf16[12,6,2,512]{3,2,1,0:T(2,128)(2,1)S(1)} %bitcast.14, bf16[4,3,6,2,512]{4,3,2,1,0:T(2,128)(2,1)S(1)} %collective-permute-done.2.over0, bf16[4,3,6,2,512]{4,3,2,1,0:T(2,128)(2,1)S(1)} %collective-permute-done.3.seam0, ...), custom_call_target="tpu_custom_call" | custom-call | flops 1073741824 | bytes 2097152 | tf_op jit(solution)/shard_map/edges/pallas_call | solution.py:335
  (1 shorter events, 0.0 us)
Async XLA Ops:
  0.0 36.4 %copy-start = (f32[8]{0:T(128)S(1)}, f32[8]{0:T(128)}, u32[]{:S(2)}) copy-start(f32[8]{0:T(128)} %scale.1) | copy-start | bytes 100
  3.5 7.2 %collective-permute-start = (bf16[12,6,2,512]{3,2,1,0:T(2,128)(2,1)S(1)}, bf16[12,6,2,512]{3,2,1,0:T(2,128)(2,1)S(1)}, u32[]{:S(2)}, u32[]{:S(2)}) collective-permute-start(bf16[12,6,2,512]{3,2,1,0:T(2,128)(2,1)S(1)} %bitcast.15), channel_id=1, source_target_pairs={{0,1},{1,0},{2,3},{3,2},{4,5},{5,4},{6,7},{7,6},{8,9},{9,8},{10,11... | collective-permute-start | bytes 442376 | tf_op jit(solution)/shard_map/ppermute | solution.py:363
  6.1 8.6 %collective-permute-start.1 = (bf16[12,6,2,512]{3,2,1,0:T(2,128)(2,1)S(1)}, bf16[12,6,2,512]{3,2,1,0:T(2,128)(2,1)S(1)}, u32[]{:S(2)}, u32[]{:S(2)}) collective-permute-start(bf16[12,6,2,512]{3,2,1,0:T(2,128)(2,1)S(1)} %bitcast.18), channel_id=1, source_target_pairs={{0,31},{1,2},{2,1},{3,4},{4,3},{5,6},{6,5},{7,8},{8,7},{9,10},{10,... | collective-permute-start | bytes 442376 | tf_op jit(solution)/shard_map/ppermute | solution.py:363
  14.7 25.1 %collective-permute-start.2 = (bf16[4,3,6,2,512]{4,3,2,1,0:T(2,128)(2,1)S(1)}, bf16[4,3,6,2,512]{4,3,2,1,0:T(2,128)(2,1)S(1)}, u32[]{:S(2)}, u32[]{:S(2)}) collective-permute-start(bf16[4,3,6,2,512]{4,3,2,1,0:T(2,128)(2,1)S(1)} %get-tuple-element.21), channel_id=1, source_target_pairs={{0,32},{32,0},{64,96},{96,64},{128,160},{160,128},{192,224},{224,1... | collective-permute-start | bytes 442376 | tf_op jit(solution)/shard_map/ppermute | solution.py:363
  18.7 21.1 %collective-permute-start.3 = (bf16[4,3,6,2,512]{4,3,2,1,0:T(2,128)(2,1)S(1)}, bf16[4,3,6,2,512]{4,3,2,1,0:T(2,128)(2,1)S(1)}, u32[]{:S(2)}, u32[]{:S(2)}) collective-permute-start(bf16[4,3,6,2,512]{4,3,2,1,0:T(2,128)(2,1)S(1)} %get-tuple-element.21), channel_id=1, source_target_pairs={{448,480},{480,448},{449,481},{481,449},{450,482},{482,450},{451,4... | collective-permute-start | bytes 442376 | tf_op jit(solution)/shard_map/ppermute | solution.py:363
  19.4 20.4 %collective-permute-start.4 = (bf16[4,3,6,2,512]{4,3,2,1,0:T(2,128)(2,1)S(1)}, bf16[4,3,6,2,512]{4,3,2,1,0:T(2,128)(2,1)S(1)}, u32[]{:S(2)}, u32[]{:S(2)}) collective-permute-start(bf16[4,3,6,2,512]{4,3,2,1,0:T(2,128)(2,1)S(1)} %get-tuple-element.22), channel_id=1, source_target_pairs={{0,0},{32,64},{64,32},{96,128},{128,96},{160,192},{192,160},{224,2... | collective-permute-start | bytes 442376 | tf_op jit(solution)/shard_map/ppermute | solution.py:363

commit v6 on v5

--- a/solution.py
+++ b/solution.py
@@ -201,37 +201,44 @@
     return bf16(result)
 
 
-def middle_kernel(own0, own1, mine0, mine1, beside0, beside1, weight, scale, projection, *refs):
-    made, keys, values, queries, out_weight, blended, sent = refs
+def query_kernel(mine0, mine1, weight, scale, queries):
+    lat = lax.axis_index("lat")
+    ones = head_ones()
+    asking = [pairs_of(mine[pl.ds(EDGE, ROWS - 2 * EDGE)]) for mine in (mine0, mine1)]
+    for edge in (0, 1):
+        for mine in (mine0, mine1):
+            asking += [pairs_of(mine[pl.ds(edge_start(edge, lat), EDGE)]), asking[0][:2]]
+    asking = flat(jnp.concatenate(asking, axis=0))
+    for group in (0, 1):
+        queries[:, 256 * group : 256 * group + 256] = scaled_queries(asking, weight, group, scale, ones)
+
+
+def middle_kernel(own0, own1, mine0, mine1, beside0, beside1, weight, projection, queries, *refs):
+    made, keys, values, out_weight, blended, sent = refs
     lat, lon = lax.axis_index("lat"), lax.axis_index("lon")
     middle = pl.ds(EDGE, ROWS - 2 * EDGE)
     ones = head_ones()
     fetched = pltpu.make_async_copy(projection, out_weight, sent)
     fetched.start()
-    every, asking = [], []
+    every = []
     for mine, beside in ((mine0, beside0), (mine1, beside1)):
-        asking.append(pairs_of(mine[middle]))
-        every += [asking[-1], pairs_of(beside[middle])]
+        every += [pairs_of(mine[middle]), pairs_of(beside[middle])]
     for edge in (0, 1):
         rows = pl.ds(edge_start(edge, lat), EDGE)
         for mine, beside in ((mine0, beside0), (mine1, beside1)):
-            asking += [pairs_of(mine[rows]), asking[0][:2]]
             every += [pairs_of(mine[rows]), pairs_of(beside[rows])]
     every = flat(jnp.concatenate(every, axis=0))
-    asking = flat(jnp.concatenate(asking, axis=0))
     for group in (0, 1):
         lanes = slice(256 * group, 256 * group + 256)
-        query = scaled_queries(asking, weight, group, scale, ones)
         key = unit(every, weight, D + 256 * group, ones)
         value = projected(every, weight, 2 * D + 256 * group)
         for half in (0, 1):
             window = slice(144 * half, 144 * half + 144)
             blended[72 * half : 72 * half + 72, lanes] = attended(
-                query[72 * half : 72 * half + 72], bf16(key[window]), value[window]
+                queries[72 * half : 72 * half + 72, lanes], bf16(key[window]), value[window]
             )
         keys[:, lanes] = key[288:]
         values[:, lanes] = value[288:].astype(jnp.float32)
-        queries[:, lanes] = query[144:]
     tokens = [flat(own[middle]).astype(jnp.float32) for own in (own0, own1)]
     fetched.wait()
     result = jnp.concatenate(tokens, axis=0) + dot(blended[...], out_weight[...])
@@ -266,7 +273,7 @@
         for at in range(4):
             far = slice(72 * at, 72 * at + 72)
             blended[40 * at : 40 * at + 40, lanes] = attended(
-                queries[40 * at : 40 * at + 40, lanes],
+                queries[144 + 40 * at : 184 + 40 * at, lanes],
                 bf16(jnp.concatenate([keys[far, lanes], key[far]], axis=0)),
                 bf16(jnp.concatenate([values[far, lanes], value[far]], axis=0)),
                 live if at >= 2 else None,
@@ -305,18 +312,29 @@
     )(*mine, *beside)
 
 
-def middle_windows(own, mine, beside, qkv_weight, logit_scale, out_weight):
+def own_queries(mine, qkv_weight, logit_scale):
+    return pl.pallas_call(
+        query_kernel,
+        out_shape=jax.ShapeDtypeStruct((304, D), jnp.float32),
+        in_specs=[VMEM] * 3 + [SMEM],
+        out_specs=VMEM,
+        compiler_params=pltpu.CompilerParams(vmem_limit_bytes=16 * MIB),
+        cost_estimate=pl.CostEstimate(flops=1 << 28, bytes_accessed=MIB, transcendentals=0),
+        name="queries",
+    )(*mine, qkv_weight, logit_scale)
+
+
+def middle_windows(own, mine, beside, qkv_weight, out_weight, queries):
     return pl.pallas_call(
         middle_kernel,
         out_shape=(
             jax.ShapeDtypeStruct((6, COLS, Z, D), jnp.float32),
             jax.ShapeDtypeStruct((288, D), jnp.float32),
             jax.ShapeDtypeStruct((288, D), jnp.float32),
-            jax.ShapeDtypeStruct((160, D), jnp.float32),
             jax.ShapeDtypeStruct((D, D), jnp.bfloat16),
         ),
-        in_specs=[VMEM] * 7 + [SMEM, HBM],
-        out_specs=(VMEM,) * 5,
+        in_specs=[VMEM] * 7 + [HBM, VMEM],
+        out_specs=(VMEM,) * 4,
         scratch_shapes=[pltpu.VMEM((144, D), jnp.bfloat16), pltpu.SemaphoreType.DMA(())],
         compiler_params=pltpu.CompilerParams(vmem_limit_bytes=32 * MIB),
         cost_estimate=pl.CostEstimate(flops=2 << 30, bytes_accessed=2 * MIB, transcendentals=350000),
@@ -326,8 +344,8 @@
         *mine,
         *beside,
         qkv_weight,
-        logit_scale,
         pltpu.with_memory_space_constraint(out_weight, pltpu.HBM),
+        queries,
     )
 
 
@@ -378,6 +396,7 @@
     own, mine, qkv_weight = expand(
         coarse, skip_tokens, land_sea, surf_table, expand_weight, expand_gain, attn_gain, qkv_weight
     )
+    queries = own_queries(mine, qkv_weight, logit_scale)
     beside = []
     for turn in (0, 1):
         beside.append(swapped(mine[turn], "lon", turn, True))
@@ -388,7 +407,7 @@
     over1 = swapped(rows[1], "lat", 1, False)
     seam0 = swapped(rows[0], "lat", 0, False, at_seam)
     over = (over0, seam0, over1)
-    begun, keys, values, queries, out_weight = middle_windows(own, mine, beside, qkv_weight, logit_scale, out_weight)
+    begun, keys, values, out_weight = middle_windows(own, mine, beside, qkv_weight, out_weight, queries)
     mixed = edge_windows(own, over, qkv_weight, begun, keys, values, queries, out_weight)
     return jnp.transpose(mixed, (2, 0, 1, 3))
 

time: 42.3 us -> 41.8 us (0.988)
  the two profiles are of different devices: /device:TPU:31 before, /device:TPU:47 now
where the time goes in v6:
time: 41.8 us; the launch traced here: 41.6 us
  starting transfers between devices  26.7 us (64%)
  Pallas kernels  9.38 us (22%)
  waiting for transfers between devices  5.38 us (13%)
    ppermute x5, starting transfers between devices, swapped(): return lax.ppermute(value, axis, pairs)  26.7 us
    ppermute x5, waiting for transfers between devices, swapped(): return lax.ppermute(value, axis, pairs)  5.38 us
    pallas_call x1, Pallas kernels, expand(): pl.pallas_call(expand_kernel, out_shape=(half,) * 4 + (jax.ShapeDtypeStru...  3.53 us
    pallas_call x1, Pallas kernels, middle_windows(): pl.pallas_call(middle_kernel, out_shape=(jax.ShapeDtypeStruct((6, COLS, Z...  2.35 us
    pallas_call x1, Pallas kernels, edge_windows(): pl.pallas_call(edge_kernel, out_shape=jax.ShapeDtypeStruct((ROWS, COLS, Z...  2.23 us
    pallas_call x1, Pallas kernels, own_queries(): pl.pallas_call(query_kernel, out_shape=jax.ShapeDtypeStruct((304, D), jnp...  1.26 us
  transfers between devices with their start and end apart: 5, of which 2 were waited for; matrix products, arithmetic and copies ran while one was open for 0% of the time, Pallas kernels for 9%

profile of v6, /device:TPU:47, one launch (start us, length us, event | category | flops | bytes accessed | tf_op | source)
XLA Modules:
  0.0 41.6 jit_solution(8803321271710251010)
XLA Ops:
  0.0 0.0 copy-start
  0.0 3.5 %expand.1 = (bf16[6,2,3,2,2,512]{5,4,3,2,1,0:T(2,128)(2,1)S(1)}, bf16[6,2,3,2,2,512]{5,4,3,2,1,0:T(2,128)(2,1)S(1)}, bf16[6,2,3,2,2,512]{5,4,3,2,1,0:T(2,128)(2,...) custom-call(bf16[6,6,2,1024]{3,2,1,0:T(2,128)(2,1)} %bitcast.24, bf16[1024,2048]{1,0:T(8,128)(2,1)} %weight.1, ...), custom_call_target="tpu_custom_call" | custom-call | flops 301989888 | bytes 5242880 | tf_op jit(solution)/shard_map/expand/pallas_call | solution.py:121
  3.5 2.6 %collective-permute-start = (bf16[12,6,2,512]{3,2,1,0:T(2,128)(2,1)S(1)}, bf16[12,6,2,512]{3,2,1,0:T(2,128)(2,1)S(1)}, u32[]{:S(2)}, u32[]{:S(2)}) collective-permute-start(bf16[12,6,2,512]{3,2,1,0:T(2,128)(2,1)S(1)} %bitcast.11), channel_id=1, source_target_pairs={{0,1},{1,0},{2,3},{3,2},{4,5},{5,4},{6,7},{7,6},{8,9},{9,8},{10,11... | collective-permute-start | bytes 442376 | tf_op jit(solution)/shard_map/ppermute | solution.py:381
  6.1 2.5 %collective-permute-start.1 = (bf16[12,6,2,512]{3,2,1,0:T(2,128)(2,1)S(1)}, bf16[12,6,2,512]{3,2,1,0:T(2,128)(2,1)S(1)}, u32[]{:S(2)}, u32[]{:S(2)}) collective-permute-start(bf16[12,6,2,512]{3,2,1,0:T(2,128)(2,1)S(1)} %bitcast.15), channel_id=1, source_target_pairs={{0,31},{1,2},{2,1},{3,4},{4,3},{5,6},{6,5},{7,8},{8,7},{9,10},{10,... | collective-permute-start | bytes 442376 | tf_op jit(solution)/shard_map/ppermute | solution.py:381
  8.6 0.0 copy-done
  8.6 1.3 %queries.1 = f32[304,512]{1,0:T(8,128)S(1)} custom-call(bf16[12,6,2,512]{3,2,1,0:T(2,128)(2,1)S(1)} %bitcast.12, bf16[12,6,2,512]{3,2,1,0:T(2,128)(2,1)S(1)} %bitcast.16, bf16[512,1536]{1,0:T(8,128)(2,1)S(1)} %get-tuple-element.22.weight, f32[8]{0:T(128)S(1)} %copy-done), custom_call_target="tpu_custom_call" | custom-call | flops 268435456 | bytes 1048576 | tf_op jit(solution)/shard_map/queries/pallas_call | solution.py:316
  9.9 0.0 collective-permute-done.beside0
  9.9 3.6 %collective-permute-done.1.beside1 = bf16[12,6,2,512]{3,2,1,0:T(2,128)(2,1)S(1)} collective-permute-done((bf16[12,6,2,512]{3,2,1,0:T(2,128)(2,1)S(1)}, bf16[12,6,2,512]{3,2,1,0:T(2,128)(2,1)S(1)}, u32[]{:S(2)}, u32[]{:S(2)}) %collective-permute-start.1) | collective-permute-done | bytes 147488 | tf_op jit(solution)/shard_map/ppermute | solution.py:381
  13.5 4.0 %collective-permute-start.2 = (bf16[4,3,6,2,512]{4,3,2,1,0:T(2,128)(2,1)S(1)}, bf16[4,3,6,2,512]{4,3,2,1,0:T(2,128)(2,1)S(1)}, u32[]{:S(2)}, u32[]{:S(2)}) collective-permute-start(bf16[4,3,6,2,512]{4,3,2,1,0:T(2,128)(2,1)S(1)} %get-tuple-element.20), channel_id=1, source_target_pairs={{0,32},{32,0},{64,96},{96,64},{128,160},{160,128},{192,224},{224,1... | collective-permute-start | bytes 442376 | tf_op jit(solution)/shard_map/ppermute | solution.py:381
  17.5 0.7 %collective-permute-start.3 = (bf16[4,3,6,2,512]{4,3,2,1,0:T(2,128)(2,1)S(1)}, bf16[4,3,6,2,512]{4,3,2,1,0:T(2,128)(2,1)S(1)}, u32[]{:S(2)}, u32[]{:S(2)}) collective-permute-start(bf16[4,3,6,2,512]{4,3,2,1,0:T(2,128)(2,1)S(1)} %get-tuple-element.20), channel_id=1, source_target_pairs={{448,480},{480,448},{449,481},{481,449},{450,482},{482,450},{451,4... | collective-permute-start | bytes 442376 | tf_op jit(solution)/shard_map/ppermute | solution.py:381
  18.2 17.0 %collective-permute-start.4 = (bf16[4,3,6,2,512]{4,3,2,1,0:T(2,128)(2,1)S(1)}, bf16[4,3,6,2,512]{4,3,2,1,0:T(2,128)(2,1)S(1)}, u32[]{:S(2)}, u32[]{:S(2)}) collective-permute-start(bf16[4,3,6,2,512]{4,3,2,1,0:T(2,128)(2,1)S(1)} %get-tuple-element.21), channel_id=1, source_target_pairs={{0,0},{32,64},{64,32},{96,128},{128,96},{160,192},{192,160},{224,2... | collective-permute-start | bytes 442376 | tf_op jit(solution)/shard_map/ppermute | solution.py:381
  35.2 2.3 %middle.1 = (f32[6,12,2,512]{3,2,1,0:T(2,128)S(1)}, f32[288,512]{1,0:T(8,128)S(1)}, f32[288,512]{1,0:T(8,128)S(1)}, bf16[512,512]{1,0:T(8,128)(2,1)S(1)}) custom-call(bf16[12,6,2,512]{3,2,1,0:T(2,128)(2,1)S(1)} %bitcast.19, bf16[12,6,2,512]{3,2,1,0:T(2,128)(2,1)S(1)} %bitcast.21, bf16[12,6,2,512]{3,2,1,0:T(2,128)(2,1)S(1)} %bitcast.14, ...), custom_call_target="tpu_custom_call" | custom-call | flops 2147483648 | bytes 2097152 | tf_op jit(solution)/shard_map/middle/pallas_call | solution.py:328
  37.5 0.0 collective-permute-done.2.over0
  37.5 0.0 collective-permute-done.3.seam0
  37.6 1.8 %collective-permute-done.4.over1 = bf16[4,3,6,2,512]{4,3,2,1,0:T(2,128)(2,1)S(1)} collective-permute-done((bf16[4,3,6,2,512]{4,3,2,1,0:T(2,128)(2,1)S(1)}, bf16[4,3,6,2,512]{4,3,2,1,0:T(2,128)(2,1)S(1)}, u32[]{:S(2)}, u32[]{:S(2)}) %collective-permute-start.4) | collective-permute-done | bytes 147488 | tf_op jit(solution)/shard_map/ppermute | solution.py:381
  39.3 2.2 %edges.1 = f32[12,12,2,512]{3,2,1,0:T(2,128)} custom-call(bf16[12,6,2,512]{3,2,1,0:T(2,128)(2,1)S(1)} %bitcast.20, bf16[12,6,2,512]{3,2,1,0:T(2,128)(2,1)S(1)} %bitcast.22, bf16[4,3,6,2,512]{4,3,2,1,0:T(2,128)(2,1)S(1)} %collective-permute-done.2.over0, bf16[4,3,6,2,512]{4,3,2,1,0:T(2,128)(2,1)S(1)} %collective-permute-done.3.seam0, ...), custom_call_target="tpu_custom_call" | custom-call | flops 1073741824 | bytes 2097152 | tf_op jit(solution)/shard_map/edges/pallas_call | solution.py:353
  (1 shorter events, 0.0 us)
Async XLA Ops:
  0.0 8.6 %copy-start = (f32[8]{0:T(128)S(1)}, f32[8]{0:T(128)}, u32[]{:S(2)}) copy-start(f32[8]{0:T(128)} %scale.1) | copy-start | bytes 100
  3.5 6.4 %collective-permute-start = (bf16[12,6,2,512]{3,2,1,0:T(2,128)(2,1)S(1)}, bf16[12,6,2,512]{3,2,1,0:T(2,128)(2,1)S(1)}, u32[]{:S(2)}, u32[]{:S(2)}) collective-permute-start(bf16[12,6,2,512]{3,2,1,0:T(2,128)(2,1)S(1)} %bitcast.11), channel_id=1, source_target_pairs={{0,1},{1,0},{2,3},{3,2},{4,5},{5,4},{6,7},{7,6},{8,9},{9,8},{10,11... | collective-permute-start | bytes 442376 | tf_op jit(solution)/shard_map/ppermute | solution.py:381
  6.1 7.4 %collective-permute-start.1 = (bf16[12,6,2,512]{3,2,1,0:T(2,128)(2,1)S(1)}, bf16[12,6,2,512]{3,2,1,0:T(2,128)(2,1)S(1)}, u32[]{:S(2)}, u32[]{:S(2)}) collective-permute-start(bf16[12,6,2,512]{3,2,1,0:T(2,128)(2,1)S(1)} %bitcast.15), channel_id=1, source_target_pairs={{0,31},{1,2},{2,1},{3,4},{4,3},{5,6},{6,5},{7,8},{8,7},{9,10},{10,... | collective-permute-start | bytes 442376 | tf_op jit(solution)/shard_map/ppermute | solution.py:381
  13.5 24.0 %collective-permute-start.2 = (bf16[4,3,6,2,512]{4,3,2,1,0:T(2,128)(2,1)S(1)}, bf16[4,3,6,2,512]{4,3,2,1,0:T(2,128)(2,1)S(1)}, u32[]{:S(2)}, u32[]{:S(2)}) collective-permute-start(bf16[4,3,6,2,512]{4,3,2,1,0:T(2,128)(2,1)S(1)} %get-tuple-element.20), channel_id=1, source_target_pairs={{0,32},{32,0},{64,96},{96,64},{128,160},{160,128},{192,224},{224,1... | collective-permute-start | bytes 442376 | tf_op jit(solution)/shard_map/ppermute | solution.py:381
  17.5 20.0 %collective-permute-start.3 = (bf16[4,3,6,2,512]{4,3,2,1,0:T(2,128)(2,1)S(1)}, bf16[4,3,6,2,512]{4,3,2,1,0:T(2,128)(2,1)S(1)}, u32[]{:S(2)}, u32[]{:S(2)}) collective-permute-start(bf16[4,3,6,2,512]{4,3,2,1,0:T(2,128)(2,1)S(1)} %get-tuple-element.20), channel_id=1, source_target_pairs={{448,480},{480,448},{449,481},{481,449},{450,482},{482,450},{451,4... | collective-permute-start | bytes 442376 | tf_op jit(solution)/shard_map/ppermute | solution.py:381
  18.2 21.1 %collective-permute-start.4 = (bf16[4,3,6,2,512]{4,3,2,1,0:T(2,128)(2,1)S(1)}, bf16[4,3,6,2,512]{4,3,2,1,0:T(2,128)(2,1)S(1)}, u32[]{:S(2)}, u32[]{:S(2)}) collective-permute-start(bf16[4,3,6,2,512]{4,3,2,1,0:T(2,128)(2,1)S(1)} %get-tuple-element.21), channel_id=1, source_target_pairs={{0,0},{32,64},{64,32},{96,128},{128,96},{160,192},{192,160},{224,2... | collective-permute-start | bytes 442376 | tf_op jit(solution)/shard_map/ppermute | solution.py:381
